TPU v7x, 512 devices: a whole 4x4x16 slice. The times are simulated.
512 devices in a mesh: gy: 16 (over z), gx: 32 (over x, y, core).
Axes of the slice: x: 4, y: 4, z: 16, core: 2. Of those that a mesh axis runs over, the one named last changes fastest.
Arguments:
- observed: float32 [16, 512, 4096], P(None, 'gy', 'gx'), may hold values from 0 to 20, as said below
- profiles: float32 [64, 3, 9], replicated, may hold values from 0.03 to 0.25
- tile_index: int32 [16, 32], replicated, may hold values from 0 to 63
Outputs:
- estimate: float32 [16, 512, 4096], P(None, 'gy', 'gx')
Inputs may be any that keep to these rules, and one draw needn't show every extreme that they name: `observed`: nonnegative intensities.
All inputs are finite; a program needn't handle non-finite values.
Results may differ from a plain program's by a relative error of at most 0.0003.
Values sent between devices are 32-bit elements; how exact they have to be, the bound alone decides.
A program may use at most 64 MiB of HBM per device.

v0:
```python
import jax
import jax.numpy as jnp
from jax import lax
from jax.sharding import PartitionSpec as P

ITERS = 2


WEIGHT_TV = 0.02
SMOOTHING = 0.1
DAMPING = 0.05
START_STEP = 0.5
EXACT_MODE = lax.Precision.HIGHEST


def extended(block, sides, width):
    for axis, dim in sides:
        count = lax.axis_size(axis)
        forward = [(i, i + 1) for i in range(count - 1)]
        backward = [(target, source) for source, target in forward]
        low = lax.ppermute(
            lax.slice_in_dim(block, block.shape[dim] - width, None, axis=dim), axis, forward
        )
        high = lax.ppermute(lax.slice_in_dim(block, 0, width, axis=dim), axis, backward)
        block = jnp.concatenate([low, block, high], axis=dim)
    return block


def from_behind(block, axis, distance):
    devices = range(lax.axis_size(axis))
    route = [(i - distance, i) for i in devices if i - distance in devices]
    return lax.ppermute(block, axis, route)


def band_matrix(profile, source_start, source_len, target_start, target_len, transposed):
    radius = (profile.shape[0] - 1) // 2
    source = jnp.arange(source_len)[:, None] + source_start
    target = jnp.arange(target_len)[None, :] + target_start
    distance = source - target if transposed else target - source
    offsets = jnp.arange(profile.shape[0]) - radius
    return jnp.sum(jnp.where(distance[:, :, None] == offsets, profile, 0.0), axis=2)


def apply_kernel(
    region, kernel, row_start, col_start, out_rows, out_cols, row_target, col_target, transposed
):
    layers, height, breadth = region.shape
    mix_cols = band_matrix(kernel[2], col_start, breadth, col_target, out_cols, transposed)
    along_cols = jnp.dot(
        region.reshape(layers * height, breadth), mix_cols, precision=EXACT_MODE
    ).reshape(layers, height, out_cols)
    mix_rows = band_matrix(kernel[1], row_start, height, row_target, out_rows, transposed)
    along_rows = jnp.einsum("zyx,yo->zox", along_cols, mix_rows, precision=EXACT_MODE)
    mix_depth = band_matrix(kernel[0], 0, layers, 0, layers, transposed)
    return jnp.einsum("zyx,zo->oyx", along_rows, mix_depth, precision=EXACT_MODE)


def pick_kernel(profiles, tile_index, row_pick, col_pick):
    grid_rows, grid_cols = tile_index.shape
    chosen_tile = (jnp.arange(grid_rows)[:, None] == row_pick) & (
        jnp.arange(grid_cols)[None, :] == col_pick
    )
    kernel_number = jnp.sum(jnp.where(chosen_tile, tile_index, 0))
    chosen_kernel = jnp.arange(profiles.shape[0])[:, None, None] == kernel_number
    return jnp.sum(jnp.where(chosen_kernel, profiles, 0.0), axis=0)


def variation_slope(padded, radius, first_row, first_col, total_rows, total_cols):
    height = padded.shape[1] - 2 * radius
    breadth = padded.shape[2] - 2 * radius
    window = padded[:, radius - 1 : radius + height + 1, radius - 1 : radius + breadth + 1]
    core = window[:, : height + 1, : breadth + 1]
    diff_rows = (window[:, 1:, :] - window[:, :-1, :])[:, :, : breadth + 1]
    diff_cols = (window[:, :, 1:] - window[:, :, :-1])[:, : height + 1, :]
    diff_depth = jnp.concatenate([core[1:] - core[:-1], jnp.zeros_like(core[:1])], 0)
    global_rows = first_row - 1 + jnp.arange(height + 1)
    global_cols = first_col - 1 + jnp.arange(breadth + 1)
    diff_rows = jnp.where((global_rows == total_rows - 1)[:, None], 0.0, diff_rows)
    diff_cols = jnp.where((global_cols == total_cols - 1)[None, :], 0.0, diff_cols)
    magnitude = jnp.sqrt(
        diff_depth * diff_depth
        + diff_rows * diff_rows
        + diff_cols * diff_cols
        + SMOOTHING * SMOOTHING
    )
    inside = (global_rows >= 0)[:, None] & (global_cols >= 0)[None, :]
    flux_rows = jnp.where(inside, diff_rows / magnitude, 0.0)
    flux_cols = jnp.where(inside, diff_cols / magnitude, 0.0)
    flux_depth = jnp.where(inside, diff_depth / magnitude, 0.0)[:, 1:, 1:]
    result = flux_rows[:, :-1, 1:] - flux_rows[:, 1:, 1:]
    result = result + flux_cols[:, 1:, :-1] - flux_cols[:, 1:, 1:]
    depth_before = jnp.concatenate([jnp.zeros_like(flux_depth[:1]), flux_depth[:-1]], 0)
    return result + depth_before - flux_depth


def per_device(observed, profiles, tile_index):
    layers, height, breadth = observed.shape
    radius = (profiles.shape[2] - 1) // 2
    row_number = lax.axis_index("gy")
    col_number = lax.axis_index("gx")
    first_row = row_number * height
    first_col = col_number * breadth
    total_rows = lax.axis_size("gy") * height
    total_cols = lax.axis_size("gx") * breadth
    kernel = pick_kernel(profiles, tile_index, row_number, col_number)

    def slope_at(estimate):
        padded = extended(estimate, (("gy", 1), ("gx", 2)), radius)
        blurred = apply_kernel(padded, kernel, 0, 0, height, breadth, radius, radius, False)
        residual = blurred - observed
        spread = apply_kernel(
            residual, kernel, radius, radius, height + 2 * radius, breadth + 2 * radius, 0, 0, True
        )
        from_right = from_behind(spread[:, :, :radius], "gx", -1)
        from_left = from_behind(spread[:, :, breadth + radius :], "gx", 1)
        middle = spread[:, :, radius : breadth + radius]
        middle = (
            middle.at[:, :, :radius].add(from_left).at[:, :, breadth - radius :].add(from_right)
        )
        from_below = from_behind(middle[:, :radius], "gy", -1)
        from_above = from_behind(middle[:, height + radius :], "gy", 1)
        pulled = (
            middle[:, radius : height + radius]
            .at[:, :radius]
            .add(from_above)
            .at[:, height - radius :]
            .add(from_below)
        )
        smooth = variation_slope(padded, radius, first_row, first_col, total_rows, total_cols)
        return pulled + WEIGHT_TV * smooth + DAMPING * estimate

    previous = observed
    prev_descent = slope_at(previous)
    current = previous - START_STEP * prev_descent
    for iteration in range(ITERS):
        descent = slope_at(current)
        change = current - previous
        growth = descent - prev_descent
        change_sq, change_growth = lax.psum(
            (jnp.sum(change * change), jnp.sum(change * growth)), ("gy", "gx")
        )
        step_size = change_sq / change_growth
        previous, prev_descent = (current, descent)
        current = current - step_size * descent
    return current


def solution(mesh):
    in_specs = (P(None, "gy", "gx"), P(), P())
    out_specs = P(None, "gy", "gx")
    return jax.shard_map(
        per_device, mesh=mesh, in_specs=in_specs, out_specs=out_specs, check_vma=False
    )
```

profile of v0, /device:TPU:1, one launch (start us, length us, event | category | flops | bytes accessed | tf_op | source)
XLA Modules:
  0.0 398.4 jit_solution(11025380353578500066)
XLA Ops:
  0.9 4.4 %collective-permute-start = (f32[16,4,128]{2,1,0:T(4,128)S(1)}, f32[16,4,128]{2,1,0:T(4,128)S(1)}, u32[]{:S(2)}, u32[]{:S(2)}) collective-permute-start(f32[16,4,128]{2,1,0:T(4,128)S(1)} %get-tuple-element.209), channel_id=1, source_target_pairs={{0,32},{32,64},{64,96},{96,128},{128,160},{160,192},{192,224},{224... | collective-permute-start | bytes 98312 | tf_op jit(solution)/shard_map/ppermute | solution.py:21
  10.3 5.0 %collective-permute-start.2 = (f32[16,40,4]{2,1,0:T(8,128)S(1)}, f32[16,40,4]{2,1,0:T(8,128)S(1)}, u32[]{:S(2)}, u32[]{:S(2)}) collective-permute-start(f32[16,40,4]{2,1,0:T(8,128)S(1)} %get-tuple-element.203), channel_id=1, source_target_pairs={{0,1},{1,2},{2,3},{3,4},{4,5},{5,6},{6,7},{7,8},{8,9},{9,10},{10,1... | collective-permute-start | bytes 30728 | tf_op jit(solution)/shard_map/ppermute | solution.py:21
  15.4 2.9 collective-permute-start.3
  20.3 3.6 collective-permute-done.3
  36.5 3.6 scatter-add.40
  42.2 5.7 %scatter-add.41 = f32[16,40,128]{2,1,0:T(8,128)S(1)} dynamic-update-slice(f32[16,40,128]{2,1,0:T(8,128)S(1)} %scatter-add.40, f32[16,40,4]{2,1,0:T(8,128)} %slice_add_fusion.2, s32[]{:T(128)} %constant.298.clone.1, s32[]{:T(128)} %constant.298.clone.1, s32[]{:T(128)} %constant.301.clone.1) | dynamic-update-slice | bytes 20484 | tf_op jit(solution)/shard_map/scatter-add | solution.py:118
  47.9 3.5 collective-permute-start.6
  53.3 4.6 %collective-permute-done.7 = f32[16,4,128]{2,1,0:T(4,128)S(1)} collective-permute-done((f32[16,4,128]{2,1,0:T(4,128)S(1)}, f32[16,4,128]{2,1,0:T(4,128)S(1)}, u32[]{:S(2)}, u32[]{:S(2)}) %collective-permute-start.7) | collective-permute-done | bytes 32800 | tf_op jit(solution)/shard_map/ppermute | solution.py:32
  59.1 4.8 %collective-permute-start.8 = (f32[16,4,128]{2,1,0:T(4,128)S(1)}, f32[16,4,128]{2,1,0:T(4,128)S(1)}, u32[]{:S(2)}, u32[]{:S(2)}) collective-permute-start(f32[16,4,128]{2,1,0:T(4,128)S(1)} %get-tuple-element.207), channel_id=1, source_target_pairs={{0,32},{32,64},{64,96},{96,128},{128,160},{160,192},{192,224},{224... | collective-permute-start | bytes 98312 | tf_op jit(solution)/shard_map/ppermute | solution.py:21
  65.2 3.4 collective-permute-done.9
  68.8 6.7 %collective-permute-start.10 = (f32[16,40,4]{2,1,0:T(8,128)S(1)}, f32[16,40,4]{2,1,0:T(8,128)S(1)}, u32[]{:S(2)}, u32[]{:S(2)}) collective-permute-start(f32[16,40,4]{2,1,0:T(8,128)S(1)} %get-tuple-element.199), channel_id=1, source_target_pairs={{0,1},{1,2},{2,3},{3,4},{4,5},{5,6},{6,7},{7,8},{8,9},{9,10},{10,1... | collective-permute-start | bytes 30728 | tf_op jit(solution)/shard_map/ppermute | solution.py:21
  80.5 3.4 collective-permute-done.11
  97.6 3.5 scatter-add.46
  102.7 5.7 %scatter-add.49 = f32[16,40,128]{2,1,0:T(8,128)S(1)} dynamic-update-slice(f32[16,40,128]{2,1,0:T(8,128)S(1)} %scatter-add.46, f32[16,40,4]{2,1,0:T(8,128)S(1)} %slice_add_fusion.1, s32[]{:T(128)} %constant.298.clone.1, s32[]{:T(128)} %constant.298.clone.1, s32[]{:T(128)} %constant.301.clone.1) | dynamic-update-slice | bytes 20484 | tf_op jit(solution)/shard_map/scatter-add | solution.py:118
  108.4 4.1 %collective-permute-start.14 = (f32[16,4,128]{2,1,0:T(4,128)S(1)}, f32[16,4,128]{2,1,0:T(4,128)S(1)}, u32[]{:S(2)}, u32[]{:S(2)}) collective-permute-start(f32[16,4,128]{2,1,0:T(4,128)S(1)} %get-tuple-element.198), channel_id=1, source_target_pairs={{0,32},{32,64},{64,96},{96,128},{128,160},{160,192},{192,224},{224... | collective-permute-start | bytes 98312 | tf_op jit(solution)/shard_map/ppermute | solution.py:32
  114.4 3.6 collective-permute-done.15
  119.2 113.8 %all-reduce.7 = (f32[]{:T(128)}, f32[]{:T(128)}) all-reduce(f32[]{:T(128)} %get-tuple-element.152, f32[]{:T(128)} %get-tuple-element.151), channel_id=1, replica_groups=mesh['gy'=16,'gx'=32] {'gy','gx'}, use_global_device_ids=true, to_apply=%region_9.10 | all-reduce | flops 2 | bytes 16 | tf_op jit(solution)/shard_map/psum | solution.py:139
  236.9 3.3 collective-permute-done.17
  240.5 3.8 collective-permute-start.18
  249.3 3.4 collective-permute-done.19
  267.1 3.6 scatter-add.54
  272.5 5.7 %scatter-add.55 = f32[16,40,128]{2,1,0:T(8,128)S(1)} dynamic-update-slice(f32[16,40,128]{2,1,0:T(8,128)S(1)} %scatter-add.54, f32[16,40,4]{2,1,0:T(8,128)} %slice_add_fusion, s32[]{:T(128)} %constant.298.clone.1, s32[]{:T(128)} %constant.298.clone.1, s32[]{:T(128)} %constant.301.clone.1) | dynamic-update-slice | bytes 20484 | tf_op jit(solution)/shard_map/scatter-add | solution.py:118
  283.1 4.0 collective-permute-done.23
  288.2 108.2 %all-reduce.6 = (f32[]{:T(128)}, f32[]{:T(128)}) all-reduce(f32[]{:T(128)} %get-tuple-element.150, f32[]{:T(128)} %get-tuple-element.149), channel_id=1, replica_groups=mesh['gy'=16,'gx'=32] {'gy','gx'}, use_global_device_ids=true, to_apply=%region_13.14 | all-reduce | flops 2 | bytes 16 | tf_op jit(solution)/shard_map/psum | solution.py:139
  (211 shorter events, 80.2 us)
Async XLA Ops:
  0.9 8.8 %collective-permute-start = (f32[16,4,128]{2,1,0:T(4,128)S(1)}, f32[16,4,128]{2,1,0:T(4,128)S(1)}, u32[]{:S(2)}, u32[]{:S(2)}) collective-permute-start(f32[16,4,128]{2,1,0:T(4,128)S(1)} %get-tuple-element.209), channel_id=1, source_target_pairs={{0,32},{32,64},{64,96},{96,128},{128,160},{160,192},{192,224},{224... | collective-permute-start | bytes 98312 | tf_op jit(solution)/shard_map/ppermute | solution.py:21
  5.3 4.8 %collective-permute-start.1 = (f32[16,4,128]{2,1,0:T(4,128)S(1)}, f32[16,4,128]{2,1,0:T(4,128)S(1)}, u32[]{:S(2)}, u32[]{:S(2)}) collective-permute-start(f32[16,4,128]{2,1,0:T(4,128)S(1)} %get-tuple-element.210), channel_id=1, source_target_pairs={{32,0},{64,32},{96,64},{128,96},{160,128},{192,160},{224,192},{256... | collective-permute-start | bytes 98312 | tf_op jit(solution)/shard_map/ppermute | solution.py:24
  10.3 9.0 %collective-permute-start.2 = (f32[16,40,4]{2,1,0:T(8,128)S(1)}, f32[16,40,4]{2,1,0:T(8,128)S(1)}, u32[]{:S(2)}, u32[]{:S(2)}) collective-permute-start(f32[16,40,4]{2,1,0:T(8,128)S(1)} %get-tuple-element.203), channel_id=1, source_target_pairs={{0,1},{1,2},{2,3},{3,4},{4,5},{5,6},{6,7},{7,8},{8,9},{9,10},{10,1... | collective-permute-start | bytes 30728 | tf_op jit(solution)/shard_map/ppermute | solution.py:21
  15.4 8.4 %collective-permute-start.3 = (f32[16,40,4]{2,1,0:T(8,128)S(1)}, f32[16,40,4]{2,1,0:T(8,128)S(1)}, u32[]{:S(2)}, u32[]{:S(2)}) collective-permute-start(f32[16,40,4]{2,1,0:T(8,128)S(1)} %get-tuple-element.204), channel_id=1, source_target_pairs={{1,0},{2,1},{3,2},{4,3},{5,4},{6,5},{7,6},{8,7},{9,8},{10,9},{11,1... | collective-permute-start | bytes 30728 | tf_op jit(solution)/shard_map/ppermute | solution.py:24
  29.7 5.9 %collective-permute-start.4 = (f32[16,40,4]{2,1,0:T(8,128)S(1)}, f32[16,40,4]{2,1,0:T(8,128)S(1)}, u32[]{:S(2)}, u32[]{:S(2)}) collective-permute-start(f32[16,40,4]{2,1,0:T(8,128)S(1)} %copy.86), channel_id=1, source_target_pairs={{0,1},{1,2},{2,3},{3,4},{4,5},{5,6},{6,7},{7,8},{8,9},{9,10},{10,1... | collective-permute-start | bytes 30728 | tf_op jit(solution)/shard_map/ppermute | solution.py:32
  31.6 8.7 %collective-permute-start.5 = (f32[16,40,4]{2,1,0:T(8,128)}, f32[16,40,4]{2,1,0:T(8,128)}, u32[]{:S(2)}, u32[]{:S(2)}) collective-permute-start(f32[16,40,4]{2,1,0:T(8,128)} %copy.87), channel_id=1, source_target_pairs={{1,0},{2,1},{3,2},{4,3},{5,4},{6,5},{7,6},{8,7},{9,8},{10,9},{11,1... | collective-permute-start | bytes 30728 | tf_op jit(solution)/shard_map/ppermute | solution.py:32
  47.9 5.3 %collective-permute-start.6 = (f32[16,4,128]{2,1,0:T(4,128)S(1)}, f32[16,4,128]{2,1,0:T(4,128)S(1)}, u32[]{:S(2)}, u32[]{:S(2)}) collective-permute-start(f32[16,4,128]{2,1,0:T(4,128)S(1)} %get-tuple-element.202), channel_id=1, source_target_pairs={{0,32},{32,64},{64,96},{96,128},{128,160},{160,192},{192,224},{224... | collective-permute-start | bytes 98312 | tf_op jit(solution)/shard_map/ppermute | solution.py:32
  52.0 6.0 %collective-permute-start.7 = (f32[16,4,128]{2,1,0:T(4,128)S(1)}, f32[16,4,128]{2,1,0:T(4,128)S(1)}, u32[]{:S(2)}, u32[]{:S(2)}) collective-permute-start(f32[16,4,128]{2,1,0:T(4,128)S(1)} %get-tuple-element.201), channel_id=1, source_target_pairs={{32,0},{64,32},{96,64},{128,96},{160,128},{192,160},{224,192},{256... | collective-permute-start | bytes 98312 | tf_op jit(solution)/shard_map/ppermute | solution.py:32
  59.1 6.2 %collective-permute-start.8 = (f32[16,4,128]{2,1,0:T(4,128)S(1)}, f32[16,4,128]{2,1,0:T(4,128)S(1)}, u32[]{:S(2)}, u32[]{:S(2)}) collective-permute-start(f32[16,4,128]{2,1,0:T(4,128)S(1)} %get-tuple-element.207), channel_id=1, source_target_pairs={{0,32},{32,64},{64,96},{96,128},{128,160},{160,192},{192,224},{224... | collective-permute-start | bytes 98312 | tf_op jit(solution)/shard_map/ppermute | solution.py:21
  63.9 4.7 %collective-permute-start.9 = (f32[16,4,128]{2,1,0:T(4,128)S(1)}, f32[16,4,128]{2,1,0:T(4,128)S(1)}, u32[]{:S(2)}, u32[]{:S(2)}) collective-permute-start(f32[16,4,128]{2,1,0:T(4,128)S(1)} %get-tuple-element.208), channel_id=1, source_target_pairs={{32,0},{64,32},{96,64},{128,96},{160,128},{192,160},{224,192},{256... | collective-permute-start | bytes 98312 | tf_op jit(solution)/shard_map/ppermute | solution.py:24
  68.8 10.7 %collective-permute-start.10 = (f32[16,40,4]{2,1,0:T(8,128)S(1)}, f32[16,40,4]{2,1,0:T(8,128)S(1)}, u32[]{:S(2)}, u32[]{:S(2)}) collective-permute-start(f32[16,40,4]{2,1,0:T(8,128)S(1)} %get-tuple-element.199), channel_id=1, source_target_pairs={{0,1},{1,2},{2,3},{3,4},{4,5},{5,6},{6,7},{7,8},{8,9},{9,10},{10,1... | collective-permute-start | bytes 30728 | tf_op jit(solution)/shard_map/ppermute | solution.py:21
  75.5 8.4 %collective-permute-start.11 = (f32[16,40,4]{2,1,0:T(8,128)S(1)}, f32[16,40,4]{2,1,0:T(8,128)S(1)}, u32[]{:S(2)}, u32[]{:S(2)}) collective-permute-start(f32[16,40,4]{2,1,0:T(8,128)S(1)} %get-tuple-element.200), channel_id=1, source_target_pairs={{1,0},{2,1},{3,2},{4,3},{5,4},{6,5},{7,6},{8,7},{9,8},{10,9},{11,1... | collective-permute-start | bytes 30728 | tf_op jit(solution)/shard_map/ppermute | solution.py:24
  90.8 6.7 %collective-permute-start.12 = (f32[16,40,4]{2,1,0:T(8,128)S(1)}, f32[16,40,4]{2,1,0:T(8,128)S(1)}, u32[]{:S(2)}, u32[]{:S(2)}) collective-permute-start(f32[16,40,4]{2,1,0:T(8,128)S(1)} %copy.90), channel_id=1, source_target_pairs={{0,1},{1,2},{2,3},{3,4},{4,5},{5,6},{6,7},{7,8},{8,9},{9,10},{10,1... | collective-permute-start | bytes 30728 | tf_op jit(solution)/shard_map/ppermute | solution.py:32
  92.7 8.8 %collective-permute-start.13 = (f32[16,40,4]{2,1,0:T(8,128)}, f32[16,40,4]{2,1,0:T(8,128)}, u32[]{:S(2)}, u32[]{:S(2)}) collective-permute-start(f32[16,40,4]{2,1,0:T(8,128)} %copy.91), channel_id=1, source_target_pairs={{1,0},{2,1},{3,2},{4,3},{5,4},{6,5},{7,6},{8,7},{9,8},{10,9},{11,1... | collective-permute-start | bytes 30728 | tf_op jit(solution)/shard_map/ppermute | solution.py:32
  108.4 6.0 %collective-permute-start.14 = (f32[16,4,128]{2,1,0:T(4,128)S(1)}, f32[16,4,128]{2,1,0:T(4,128)S(1)}, u32[]{:S(2)}, u32[]{:S(2)}) collective-permute-start(f32[16,4,128]{2,1,0:T(4,128)S(1)} %get-tuple-element.198), channel_id=1, source_target_pairs={{0,32},{32,64},{64,96},{96,128},{128,160},{160,192},{192,224},{224... | collective-permute-start | bytes 98312 | tf_op jit(solution)/shard_map/ppermute | solution.py:32
  113.0 5.1 %collective-permute-start.15 = (f32[16,4,128]{2,1,0:T(4,128)S(1)}, f32[16,4,128]{2,1,0:T(4,128)S(1)}, u32[]{:S(2)}, u32[]{:S(2)}) collective-permute-start(f32[16,4,128]{2,1,0:T(4,128)S(1)} %get-tuple-element.197), channel_id=1, source_target_pairs={{32,0},{64,32},{96,64},{128,96},{160,128},{192,160},{224,192},{256... | collective-permute-start | bytes 98312 | tf_op jit(solution)/shard_map/ppermute | solution.py:32
  234.3 2.6 collective-permute-start.16
  235.6 4.7 %collective-permute-start.17 = (f32[16,4,128]{2,1,0:T(4,128)S(1)}, f32[16,4,128]{2,1,0:T(4,128)S(1)}, u32[]{:S(2)}, u32[]{:S(2)}) collective-permute-start(f32[16,4,128]{2,1,0:T(4,128)S(1)} %get-tuple-element.206), channel_id=1, source_target_pairs={{32,0},{64,32},{96,64},{128,96},{160,128},{192,160},{224,192},{256... | collective-permute-start | bytes 98312 | tf_op jit(solution)/shard_map/ppermute | solution.py:24
  240.5 7.8 %collective-permute-start.18 = (f32[16,40,4]{2,1,0:T(8,128)S(1)}, f32[16,40,4]{2,1,0:T(8,128)S(1)}, u32[]{:S(2)}, u32[]{:S(2)}) collective-permute-start(f32[16,40,4]{2,1,0:T(8,128)S(1)} %get-tuple-element.195), channel_id=1, source_target_pairs={{0,1},{1,2},{2,3},{3,4},{4,5},{5,6},{6,7},{7,8},{8,9},{9,10},{10,1... | collective-permute-start | bytes 30728 | tf_op jit(solution)/shard_map/ppermute | solution.py:21
  244.3 8.4 %collective-permute-start.19 = (f32[16,40,4]{2,1,0:T(8,128)S(1)}, f32[16,40,4]{2,1,0:T(8,128)S(1)}, u32[]{:S(2)}, u32[]{:S(2)}) collective-permute-start(f32[16,40,4]{2,1,0:T(8,128)S(1)} %get-tuple-element.196), channel_id=1, source_target_pairs={{1,0},{2,1},{3,2},{4,3},{5,4},{6,5},{7,6},{8,7},{9,8},{10,9},{11,1... | collective-permute-start | bytes 30728 | tf_op jit(solution)/shard_map/ppermute | solution.py:24
  259.5 6.7 %collective-permute-start.20 = (f32[16,40,4]{2,1,0:T(8,128)S(1)}, f32[16,40,4]{2,1,0:T(8,128)S(1)}, u32[]{:S(2)}, u32[]{:S(2)}) collective-permute-start(f32[16,40,4]{2,1,0:T(8,128)S(1)} %copy.94), channel_id=1, source_target_pairs={{0,1},{1,2},{2,3},{3,4},{4,5},{5,6},{6,7},{7,8},{8,9},{9,10},{10,1... | collective-permute-start | bytes 30728 | tf_op jit(solution)/shard_map/ppermute | solution.py:32
  261.4 9.2 %collective-permute-start.21 = (f32[16,40,4]{2,1,0:T(8,128)}, f32[16,40,4]{2,1,0:T(8,128)}, u32[]{:S(2)}, u32[]{:S(2)}) collective-permute-start(f32[16,40,4]{2,1,0:T(8,128)} %copy.95), channel_id=1, source_target_pairs={{1,0},{2,1},{3,2},{4,3},{5,4},{6,5},{7,6},{8,7},{9,8},{10,9},{11,1... | collective-permute-start | bytes 30728 | tf_op jit(solution)/shard_map/ppermute | solution.py:32
  278.3 4.8 %collective-permute-start.22 = (f32[16,4,128]{2,1,0:T(4,128)S(1)}, f32[16,4,128]{2,1,0:T(4,128)S(1)}, u32[]{:S(2)}, u32[]{:S(2)}) collective-permute-start(f32[16,4,128]{2,1,0:T(4,128)S(1)} %get-tuple-element.194), channel_id=1, source_target_pairs={{0,32},{32,64},{64,96},{96,128},{128,160},{160,192},{192,224},{224... | collective-permute-start | bytes 98312 | tf_op jit(solution)/shard_map/ppermute | solution.py:32
  281.6 5.4 %collective-permute-start.23 = (f32[16,4,128]{2,1,0:T(4,128)S(1)}, f32[16,4,128]{2,1,0:T(4,128)S(1)}, u32[]{:S(2)}, u32[]{:S(2)}) collective-permute-start(f32[16,4,128]{2,1,0:T(4,128)S(1)} %get-tuple-element.193), channel_id=1, source_target_pairs={{32,0},{64,32},{96,64},{128,96},{160,128},{192,160},{224,192},{256... | collective-permute-start | bytes 98312 | tf_op jit(solution)/shard_map/ppermute | solution.py:32
  (34 other events, 355.5 us)
where the time goes:
time: 400 us; the launch traced here: 398 us
  blocking collectives  222 us (56%)
  starting transfers between devices  64.8 us (16%)
  local copies, waits for them, and re-layouts  40.1 us (10%)
  waiting for transfers between devices  35.8 us (9%)
  other arithmetic  20.8 us (5%)
  matrix products  11.2 us (3%)
    psum x2, blocking collectives, per_device(): lax.psum((jnp.sum(change * change), jnp.sum(change * growth)), ('gy', 'gx'))  222 us
    scatter-add x6, local copies, waits for them, and re-layouts, slope_at(): middle.at[:, :, :radius].add(from_left).at[:, :, breadth - radius:]  27.7 us
    ppermute x12, starting transfers between devices, from_behind(): return lax.ppermute(block, axis, route)  27.7 us
    ppermute x6, starting transfers between devices, extended(): lax.ppermute(lax.slice_in_dim(block, block.shape[dim] - width, None, axis...  26.1 us
    ppermute x6, waiting for transfers between devices, extended(): lax.ppermute(lax.slice_in_dim(block, 0, width, axis=dim), axis, backward)  17.5 us
    ppermute x12, waiting for transfers between devices, from_behind(): return lax.ppermute(block, axis, route)  13.6 us
    ppermute x6, starting transfers between devices, extended(): lax.ppermute(lax.slice_in_dim(block, 0, width, axis=dim), axis, backward)  11.1 us
  transfers between devices with their start and end apart: 24, of which 15 were waited for; matrix products, arithmetic and copies ran while one was open for 6% of the time, Pallas kernels for 0%

commit v1 on v0

v1 whole, which is shorter than its diff:
```python
import functools

import jax
import jax.numpy as jnp
from jax import lax
from jax.experimental import pallas as pl
from jax.experimental.pallas import tpu as pltpu
from jax.sharding import PartitionSpec as P

WEIGHT_TV = 0.02
SMOOTHING = 0.1
DAMPING = 0.05
START_STEP = 0.5
RADIUS = 4
TAPS = 9
Z, CY, CX = 16, 32, 128
EXT = CY + 16
MESH = pl.DeviceIdType.MESH
F32 = jnp.float32
BF16 = jnp.bfloat16
SIDES = ((-1, 0), (1, 0), (0, -1), (0, 1), (-1, -1), (-1, 1), (1, -1), (1, 1))


def kernel(
    ny, nx,
    obs_hbm, prof, tiles, out_ref,
    u_ext, g_ext, grad, tv, resid, back, spread, blur_in, blur_y, flux,
    fwd_hi, fwd_lo, bwd_hi, bwd_lo, lhs_hi, lhs_lo,
    ux, gx_halo, own_edge, edge_pad, edge_spill,
    send_y, recv_y, send_x, recv_x,
    part, all_x, part_y, all_y,
    load_sem, send_sem, recv_sem, ar_send, ar_recv,
):
    row = lax.axis_index("gy")
    col = lax.axis_index("gx")

    def at(dy, dx):
        return {
            "gy": lax.rem(row + dy + ny, ny),
            "gx": lax.rem(col + dx + nx, nx),
        }

    load = pltpu.make_async_copy(obs_hbm, u_ext.at[:, pl.ds(8, CY), :], load_sem)
    load.start()

    barrier = pltpu.get_barrier_semaphore()

    def greet_x(i, c):
        pl.semaphore_signal(barrier, inc=1, device_id=at(0, i), device_id_type=MESH)
        return c

    def greet_y(i, c):
        pl.semaphore_signal(barrier, inc=1, device_id=at(i, 0), device_id_type=MESH)
        return c

    lax.fori_loop(1, nx, greet_x, 0)
    lax.fori_loop(1, ny, greet_y, 0)
    for dy in (-1, 1):
        for dx in (-1, 1):
            pl.semaphore_signal(barrier, inc=1, device_id=at(dy, dx), device_id_type=MESH)

    number = tiles[row, col]
    depth = [prof[a, 0, number] for a in range(TAPS)]
    along = [prof[a, 1, number] for a in range(TAPS)]
    across = [prof[a, 2, number] for a in range(TAPS)]

    lane = lax.broadcasted_iota(jnp.int32, (1, CX), 1)
    sub8 = lax.broadcasted_iota(jnp.int32, (8, CX), 0)
    low_half = sub8 < 4
    plane_of = lane // 8
    place = lane - plane_of * 8
    first_row, last_row = row == 0, row == ny - 1
    first_col, last_col = col == 0, col == nx - 1

    mk = lax.broadcasted_iota(jnp.int32, (CX, CX), 0)
    mn = lax.broadcasted_iota(jnp.int32, (CX, CX), 1)

    def band(diff, offset):
        total = jnp.zeros((CX, CX), F32)
        for c in range(TAPS):
            total = jnp.where(diff == c - offset, across[c], total)
        return total

    def wrapped(diff):
        total = jnp.zeros((CX, CX), F32)
        for c in range(TAPS):
            hit = (diff == c - RADIUS - CX) | (diff == c - RADIUS + CX)
            total = jnp.where(hit, across[c], total)
        return total

    def halves(value):
        high = value.astype(BF16)
        return high, (value - high.astype(F32)).astype(BF16)

    ahead = mn - mk
    for part_no, w in enumerate((band(ahead, RADIUS), wrapped(ahead))):
        high, low = halves(w)
        fwd_hi[pl.ds(part_no * CX, CX), :] = high
        fwd_lo[pl.ds(part_no * CX, CX), :] = low
    behind = mk - mn
    for part_no, w in enumerate((band(behind, RADIUS), wrapped(behind))):
        high, low = halves(w)
        bwd_hi[:, pl.ds(part_no * CX, CX)] = high
        bwd_lo[:, pl.ds(part_no * CX, CX)] = low

    back[:, pl.ds(0, 16), :] = jnp.zeros((Z, 16, CX), F32)
    back[:, pl.ds(16 + CY, 16), :] = jnp.zeros((Z, 16, CX), F32)
    edge_pad[pl.ds(0, 16), :] = jnp.zeros((16, CX), F32)
    edge_pad[pl.ds(16 + CY, 16), :] = jnp.zeros((16, CX), F32)

    load.wait()
    pl.semaphore_wait(barrier, nx - 1 + ny - 1 + 4)

    def planes(body, init, step=4):
        def some(i, carry):
            for k in range(step):
                carry = body(i * step + k, carry)
            return carry

        return lax.fori_loop(0, Z // step, some, init)

    def pack_columns(read):
        def body(p, total):
            turned = pltpu.roll(read(p), 8 * p + 4, 1)
            return jnp.where(plane_of == p, turned, total)

        return planes(body, jnp.zeros((CY, CX), F32))

    def copies(r):
        made = []
        for k, (dy, dx) in enumerate(SIDES):
            if dx == 0:
                src = send_y.at[r, 0 if dy < 0 else 1]
                dst = recv_y.at[r, 1 if dy < 0 else 0]
            else:
                start, size = {-1: (0, 8), 0: (8, CY), 1: (8 + CY, 8)}[dy]
                land = {-1: 8 + CY, 0: 8, 1: 0}[dy]
                src = send_x.at[r, pl.ds(start, size), :]
                dst = recv_x.at[r, 1 if dx < 0 else 0, pl.ds(land, size), :]
            made.append(
                pltpu.make_async_remote_copy(
                    src_ref=src, dst_ref=dst,
                    send_sem=send_sem.at[r, k], recv_sem=recv_sem.at[r, k],
                    device_id=at(dy, dx), device_id_type=MESH,
                )
            )
        return made

    def send(r):
        made = copies(r)
        for k in (4, 5, 6, 7, 2, 3, 0, 1):
            made[k].start()
        return made

    def halo_send(r, ext, edges_out):
        edge = pack_columns(lambda p: ext[p, pl.ds(8, CY), :])
        edges_out[...] = edge
        send_x[r, pl.ds(8, CY), :] = edge
        send_x[r, pl.ds(0, 8), :] = edge[0:8]
        send_x[r, pl.ds(8 + CY, 8), :] = edge[CY - 8 : CY]
        for q in range(8):
            top, top2 = ext[q, pl.ds(8, 8), :], ext[q + 8, pl.ds(8, 8), :]
            send_y[r, 0, q] = jnp.where(low_half, top, pltpu.roll(top2, 4, 0))
            low, low2 = ext[q, pl.ds(CY, 8), :], ext[q + 8, pl.ds(CY, 8), :]
            send_y[r, 1, q] = jnp.where(low_half, pltpu.roll(low, 4, 0), low2)
        return send(r)

    def halo_wait(r, made, ext, halo):
        for c in made:
            c.wait_recv()
        for q in range(8):
            above = jnp.where(first_row, 0.0, recv_y[r, 0, q])
            ext[q, pl.ds(0, 8), :] = pltpu.roll(above, 4, 0)
            ext[q + 8, pl.ds(0, 8), :] = above
            below = jnp.where(last_row, 0.0, recv_y[r, 1, q])
            ext[q, pl.ds(8 + CY, 8), :] = below
            ext[q + 8, pl.ds(8 + CY, 8), :] = pltpu.roll(below, 4, 0)
        halo[...] = sides(r, place < 4)

    def sides(r, from_left):
        left = jnp.where(first_col, 0.0, recv_x[r, 0])
        right = jnp.where(last_col, 0.0, recv_x[r, 1])
        both = jnp.where(from_left, left, right)
        at_row = lax.broadcasted_iota(jnp.int32, (EXT, CX), 0)
        both = jnp.where(first_row & (at_row < 8), 0.0, both)
        return jnp.where(last_row & (at_row >= 8 + CY), 0.0, both)

    def depth_blur(read, write, transposed):
        for t in range(CY // 8):
            value = [read(p, t) for p in range(Z)]
            for p in range(Z):
                total = None
                for a in range(TAPS):
                    source = p - RADIUS + a if transposed else p + RADIUS - a
                    if 0 <= source < Z:
                        term = depth[a] * value[source]
                        total = term if total is None else total + term
                write(p, t, total)

    def blur(ext, halo, write):
        edge = jnp.zeros((CY, CX), F32)
        for b in range(TAPS):
            edge = edge + along[b] * halo[pl.ds(8 + RADIUS - b, CY), :]

        def body(p, c):
            total = along[0] * ext[p, pl.ds(8 + RADIUS, CY), :]
            for b in range(1, TAPS):
                total = total + along[b] * ext[p, pl.ds(8 + RADIUS - b, CY), :]
            here = pl.ds(pl.multiple_of(p * CY, CY), CY)
            high, low = halves(total)
            lhs_hi[here, pl.ds(0, CX)] = high
            lhs_lo[here, pl.ds(0, CX)] = low
            high, low = halves(pltpu.roll(edge, 124 - 8 * p, 1))
            lhs_hi[here, pl.ds(CX, CX)] = high
            lhs_lo[here, pl.ds(CX, CX)] = low
            return c

        planes(body, 0)
        mixed = jnp.dot(lhs_hi[...], fwd_hi[...], preferred_element_type=F32)
        mixed = mixed + jnp.dot(lhs_lo[...], fwd_hi[...], preferred_element_type=F32)
        mixed = mixed + jnp.dot(lhs_hi[...], fwd_lo[...], preferred_element_type=F32)
        blur_y[:, pl.ds(0, CX)] = mixed
        depth_blur(lambda p, t: blur_y[pl.ds(p * CY + t * 8, 8), pl.ds(0, CX)], write, False)

    def spill_send(r, field):
        def keep(p, t, value):
            high, low = halves(value)
            here = pl.ds(p * CY + t * 8, 8)
            blur_in[p, pl.ds(t * 8, 8), :] = value

        depth_blur(lambda p, t: field[p, pl.ds(t * 8, 8), :], keep, True)
        whole = blur_in[...].reshape(Z * CY, CX)
        high, low = halves(whole)
        mixed = jnp.dot(high, bwd_hi[...], preferred_element_type=F32)
        mixed = mixed + jnp.dot(low, bwd_hi[...], preferred_element_type=F32)
        mixed = mixed + jnp.dot(high, bwd_lo[...], preferred_element_type=F32)
        blur_y[...] = mixed

        def split(p, total):
            here = pl.ds(pl.multiple_of(p * CY, CY), CY)
            back[p, pl.ds(16, CY), :] = blur_y[here, pl.ds(0, CX)]
            turned = pltpu.roll(blur_y[here, pl.ds(CX, CX)], 8 * p + 4, 1)
            return jnp.where(plane_of == p, turned, total)

        edge_pad[pl.ds(16, CY), :] = planes(split, jnp.zeros((CY, CX), F32))
        edge = along[0] * edge_pad[pl.ds(4, EXT), :]
        for b in range(1, TAPS):
            edge = edge + along[b] * edge_pad[pl.ds(4 + b, EXT), :]
        edge_spill[...] = edge
        send_x[r] = edge

        def body(p, c):
            total = along[0] * back[p, pl.ds(4, EXT), :]
            for b in range(1, TAPS):
                total = total + along[b] * back[p, pl.ds(4 + b, EXT), :]
            spread[p] = total
            return c

        planes(body, 0)
        for q in range(8):
            top, top2 = spread[q, pl.ds(0, 8), :], spread[q + 8, pl.ds(0, 8), :]
            send_y[r, 0, q] = jnp.where(low_half, pltpu.roll(top, 4, 0), top2)
            low, low2 = spread[q, pl.ds(8 + CY, 8), :], spread[q + 8, pl.ds(8 + CY, 8), :]
            send_y[r, 1, q] = jnp.where(low_half, low, pltpu.roll(low2, 4, 0))
        return send(r)

    def spill_wait(r, made):
        for c in made:
            c.wait_recv()
        both = sides(r, place >= 4)
        top = both[8:16] + both[0:8]
        low = both[CY : CY + 8] + both[CY + 8 : CY + 16]
        edge = jnp.concatenate([top, both[16:CY], low], axis=0)
        border = (lane < 4) | (lane >= CX - 4)
        for q in range(8):
            above = jnp.where(first_row, 0.0, recv_y[r, 0, q])
            below = jnp.where(last_row, 0.0, recv_y[r, 1, q])
            t, b = pl.ds(8, 8), pl.ds(CY, 8)
            spread[q, t, :] = spread[q, t, :] + jnp.where(low_half, above, 0.0)
            spread[q + 8, t, :] = spread[q + 8, t, :] + jnp.where(low_half, pltpu.roll(above, 4, 0), 0.0)
            spread[q, b, :] = spread[q, b, :] + jnp.where(low_half, 0.0, pltpu.roll(below, 4, 0))
            spread[q + 8, b, :] = spread[q + 8, b, :] + jnp.where(low_half, 0.0, below)

        def body(p, c):
            extra = jnp.where(border, pltpu.roll(edge, 124 - 8 * p, 1), 0.0)
            spread[p, pl.ds(8, CY), :] = spread[p, pl.ds(8, CY), :] + extra
            return c

        planes(body, 0)

    rows40 = lax.broadcasted_iota(jnp.int32, (40, CX), 0)
    rows32 = lax.broadcasted_iota(jnp.int32, (CY, CX), 0)
    no_row_diff = last_row & (rows40 == 39)
    no_row_flux = first_row & (rows40 == 7)
    no_col_diff = last_col & (lane == CX - 1)

    def inverse_size(dx, dy, dz):
        return lax.rsqrt(dx * dx + dy * dy + dz * dz + SMOOTHING * SMOOTHING)

    def variation(ext, halo, edges, write):
        here = halo[pl.ds(8, CY), :]
        dx = pltpu.roll(edges, CX - 1, 1) - here
        dy = halo[pl.ds(9, CY), :] - here
        dy = jnp.where(last_row & (rows32 == CY - 1), 0.0, dy)
        dz = jnp.where(plane_of == Z - 1, 0.0, pltpu.roll(here, CX - 8, 1) - here)
        side = jnp.where(first_col, 0.0, dx * inverse_size(dx, dy, dz))
        around = halo[pl.ds(0, 40), :]

        def body(p, before):
            u = ext[p, pl.ds(0, 40), :]
            dy = jnp.where(no_row_diff, 0.0, ext[p, pl.ds(1, 40), :] - u)
            beyond = pltpu.roll(around, 124 - 8 * p, 1)
            dx = pltpu.roll(jnp.where(lane == 0, beyond, u), CX - 1, 1) - u
            dx = jnp.where(no_col_diff, 0.0, dx)
            after = ext[jnp.minimum(p + 1, Z - 1), pl.ds(0, 40), :]
            dz = after - u
            inverse = inverse_size(dx, dy, dz)
            fy = jnp.where(no_row_flux, 0.0, dy * inverse)
            flux[...] = fy
            fx = (dx * inverse)[8:40]
            fz = (dz * inverse)[8:40]
            fx_side = pltpu.roll(side, 124 - 8 * p, 1)
            fx_before = pltpu.roll(jnp.where(lane == CX - 1, fx_side, fx), 1, 1)
            slope = (before - fz) + (flux[pl.ds(7, CY), :] - fy[8:40]) + (fx_before - fx)
            write(p, slope)
            return fz

        planes(body, jnp.zeros((CY, CX), F32), 2)

    def fold(values):
        total = jnp.zeros((1, CX), F32)
        for i, value in enumerate(values):
            v = jnp.sum(value, axis=0, keepdims=True)
            v = v + pltpu.roll(v, 64, 1)
            v = v + pltpu.roll(v, 32, 1)
            total = jnp.where(lane // 32 == i, v, total)
        return total

    def reduce_start(a, values):
        mine = fold(values)
        part[a] = mine
        all_x[a, pl.ds(col, 1)] = mine.reshape(1, 1, CX)

        def go(i, c):
            pltpu.make_async_remote_copy(
                src_ref=part.at[a], dst_ref=all_x.at[a, col],
                send_sem=ar_send.at[a, 0], recv_sem=ar_recv.at[a, 0],
                device_id=at(0, i), device_id_type=MESH,
            ).start()
            return c

        lax.fori_loop(1, nx, go, 0)

    def reduce_middle(a):
        got = all_x.at[a, pl.ds(0, nx - 1)]
        pltpu.make_async_copy(got, got, ar_recv.at[a, 0]).wait()
        mine = jnp.sum(all_x[a], axis=0)
        part_y[a] = mine
        all_y[a, pl.ds(row, 1)] = mine.reshape(1, 1, CX)

        def go(i, c):
            pltpu.make_async_remote_copy(
                src_ref=part_y.at[a], dst_ref=all_y.at[a, row],
                send_sem=ar_send.at[a, 1], recv_sem=ar_recv.at[a, 1],
                device_id=at(i, 0), device_id_type=MESH,
            ).start()
            return c

        lax.fori_loop(1, ny, go, 0)

    def reduce_end(a):
        got = all_y.at[a, pl.ds(0, ny - 1)]
        pltpu.make_async_copy(got, got, ar_recv.at[a, 1]).wait()
        total = jnp.sum(all_y[a], axis=0)
        return [jnp.sum(jnp.where(lane // 32 == i, total, 0.0), axis=1, keepdims=True) for i in range(3)]

    def rows8(value):
        return value[0:8] + value[8:16] + value[16:24] + value[24:32]

    zero8 = jnp.zeros((8, CX), F32)
    main = pl.ds(8, CY)

    waiting = []
    made = halo_send(0, u_ext, own_edge.at[0])
    waiting += made
    halo_wait(0, made, u_ext, ux)

    def keep_residual(p, t, value):
        here = pl.ds(t * 8, 8)
        resid[p, here, :] = value - u_ext[p, pl.ds(8 + t * 8, 8), :]

    blur(u_ext, ux, keep_residual)
    made = spill_send(1, resid)
    waiting += made

    def keep_tv(p, slope):
        tv[p] = slope

    variation(u_ext, ux, own_edge[0], keep_tv)
    spill_wait(1, made)

    def gradient(target):
        def body(p, c):
            target[p, main, :] = (
                spread[p, main, :] + WEIGHT_TV * tv[p] + DAMPING * u_ext[p, main, :]
            )
            return c

        planes(body, 0)

    gradient(g_ext)
    made = halo_send(2, g_ext, own_edge.at[1])
    waiting += made
    halo_wait(2, made, g_ext, gx_halo)

    def advance(step):
        def body(p, c):
            u_ext[p] = u_ext[p] - step * g_ext[p]
            return c

        planes(body, 0)
        ux[...] = ux[...] - step * gx_halo[...]
        own_edge[0] = own_edge[0] - step * own_edge[1]

    def blur_gradient():
        def keep(p, t, value):
            grad[p, pl.ds(t * 8, 8), :] = value

        blur(g_ext, gx_halo, keep)

    def sums_of_gradient():
        def body(p, c):
            g = g_ext[p, main, :]
            h = grad[p]
            return c[0] + rows8(g * g), c[1] + rows8(h * h)

        return planes(body, (zero8, zero8))

    def variation_change():
        def keep(p, slope):
            blur_in[p] = slope

        variation(u_ext, ux, own_edge[0], keep)

        def body(p, c):
            new = blur_in[p]
            c = c + rows8(g_ext[p, main, :] * (new - tv[p]))
            tv[p] = new
            return c

        return planes(body, zero8)

    advance(START_STEP)
    blur_gradient()
    gg, hh = sums_of_gradient()
    gt = variation_change()
    reduce_start(0, (gg, hh, gt))

    def body(p, c):
        resid[p] = resid[p] - START_STEP * grad[p]
        return c

    planes(body, 0)
    made = spill_send(3, resid)
    waiting += made
    reduce_middle(0)
    spill_wait(3, made)
    gradient(g_ext)
    def keep_spread(p, c):
        resid[p] = spread[p, main, :]
        return c

    planes(keep_spread, 0)
    made = halo_send(4, g_ext, own_edge.at[1])
    waiting += made
    halo_wait(4, made, g_ext, gx_halo)
    blur_gradient()
    gg, hh = sums_of_gradient()
    made = spill_send(5, grad)
    waiting += made
    g2, h2, t2 = reduce_end(0)
    change_sq = START_STEP * START_STEP * g2
    change_growth = START_STEP * START_STEP * (h2 + DAMPING * g2) - START_STEP * WEIGHT_TV * t2
    step = change_sq / change_growth

    advance(step)
    gt = variation_change()
    reduce_start(1, (gg, hh, gt))
    spill_wait(5, made)

    def last(p, c):
        pulled = resid[p] - step * spread[p, main, :]
        g_ext[p, main, :] = pulled + WEIGHT_TV * tv[p] + DAMPING * u_ext[p, main, :]
        return c

    reduce_middle(1)
    planes(last, 0)
    g2, h2, t2 = reduce_end(1)
    change_sq = step * step * g2
    change_growth = step * step * (h2 + DAMPING * g2) - step * WEIGHT_TV * t2
    step = change_sq / change_growth

    def finish(p, c):
        out_ref[p] = u_ext[p, main, :] - step * g_ext[p, main, :]
        return c

    planes(finish, 0)

    for c in waiting:
        c.wait_send()
    for a in range(2):
        got = all_x.at[a, pl.ds(0, nx - 1)]
        pltpu.make_async_copy(got, got, ar_send.at[a, 0]).wait()
        got = all_y.at[a, pl.ds(0, ny - 1)]
        pltpu.make_async_copy(got, got, ar_send.at[a, 1]).wait()


def per_device(ny, nx, observed, profiles, tile_index):
    field = pltpu.VMEM((Z, CY, CX), F32)
    extended = pltpu.VMEM((Z, EXT, CX), F32)
    rounds = 6
    scratch = [
        extended, extended, field, field, field,
        pltpu.VMEM((Z, CY + 32, CX), F32), extended, field,
        pltpu.VMEM((Z * CY, 2 * CX), F32), pltpu.VMEM((40, CX), F32),
        pltpu.VMEM((2 * CX, CX), BF16), pltpu.VMEM((2 * CX, CX), BF16),
        pltpu.VMEM((CX, 2 * CX), BF16), pltpu.VMEM((CX, 2 * CX), BF16),
        pltpu.VMEM((Z * CY, 2 * CX), BF16), pltpu.VMEM((Z * CY, 2 * CX), BF16),
        pltpu.VMEM((EXT, CX), F32), pltpu.VMEM((EXT, CX), F32),
        pltpu.VMEM((2, CY, CX), F32), pltpu.VMEM((CY + 32, CX), F32),
        pltpu.VMEM((EXT, CX), F32),
        pltpu.VMEM((rounds, 2, 8, 8, CX), F32), pltpu.VMEM((rounds, 2, 8, 8, CX), F32),
        pltpu.VMEM((rounds, EXT, CX), F32), pltpu.VMEM((rounds, 2, EXT, CX), F32),
        pltpu.VMEM((2, 1, CX), F32), pltpu.VMEM((2, nx, 1, CX), F32),
        pltpu.VMEM((2, 1, CX), F32), pltpu.VMEM((2, ny, 1, CX), F32),
        pltpu.SemaphoreType.DMA,
        pltpu.SemaphoreType.DMA((rounds, 8)), pltpu.SemaphoreType.DMA((rounds, 8)),
        pltpu.SemaphoreType.DMA((2, 2)), pltpu.SemaphoreType.DMA((2, 2)),
    ]
    return pl.pallas_call(
        functools.partial(kernel, ny, nx),
        out_shape=jax.ShapeDtypeStruct((Z, CY, CX), F32),
        in_specs=[
            pl.BlockSpec(memory_space=pl.ANY),
            pl.BlockSpec(memory_space=pltpu.SMEM),
            pl.BlockSpec(memory_space=pltpu.SMEM),
        ],
        out_specs=pl.BlockSpec(memory_space=pltpu.VMEM),
        scratch_shapes=scratch,
        compiler_params=pltpu.CompilerParams(collective_id=0, has_side_effects=True),
    )(observed, jnp.transpose(profiles, (2, 1, 0)), tile_index)


def solution(mesh):
    ny, nx = mesh.shape["gy"], mesh.shape["gx"]
    return jax.shard_map(
        functools.partial(per_device, ny, nx), mesh=mesh,
        in_specs=(P(None, "gy", "gx"), P(), P()),
        out_specs=P(None, "gy", "gx"), check_vma=False,
    )
```

time: 400 us -> 69.3 us (0.17)
  blocking collectives: 222 us -> 0 us
  Pallas kernels: 0 us -> 67.3 us
  starting transfers between devices: 64.8 us -> 0 us
  local copies, waits for them, and re-layouts: 40.1 us -> 1.67 us
  waiting for transfers between devices: 35.8 us -> 0 us
  other arithmetic: 20.8 us -> 0 us
  matrix products: 11.2 us -> 0 us
    psum x2 -> x0, blocking collectives: 222 us -> none  [per_device(): lax.psum((jnp.sum(change * change), jnp.sum(change * growth)), ('gy', 'gx'))]
    pallas_call x0 -> x1, Pallas kernels: none -> 67.3 us  [per_device(): pl.pallas_call(functools.partial(kernel, ny, nx), out_shape=jax.ShapeDtyp...]
    ppermute x24 -> x0, starting transfers between devices: 64.8 us -> none  [the longest x12 27.7 us: from_behind(): return lax.ppermute(block, axis, route)]
    ppermute x24 -> x0, waiting for transfers between devices: 35.8 us -> none  [the longest x6 17.5 us: extended(): lax.ppermute(lax.slice_in_dim(block, 0, width, axis=dim), axis, backward)]
    scatter-add x6 -> x0, local copies, waits for them, and re-layouts: 27.7 us -> none  [slope_at(): middle.at[:, :, :radius].add(from_left).at[:, :, breadth - radius:]]
    dot_general x18 -> x0, matrix products: 11.2 us -> none  [the longest x6 4.25 us: apply_kernel(): jnp.einsum('zyx,zo->oyx', along_rows, mix_depth, precision=EXACT_MODE)]
    add x8 -> x0, other arithmetic: 6.65 us -> none  [the longest x6 6.65 us: slope_at(): middle.at[:, :, :radius].add(from_left).at[:, :, breadth - radius:]]
    unnamed x77 -> x1, local copies, waits for them, and re-layouts: 7.22 us -> 1.67 us
  transfers between devices with their start and end apart: 24 -> 0, of which waited for: 15 -> 0; matrix products, arithmetic and copies ran while one was open for 6% -> 0% of each run, Pallas kernels for 0% -> 0%
where the time goes in v1:
time: 69.3 us; the launch traced here: 69 us
  Pallas kernels  67.3 us (97%)
  local copies, waits for them, and re-layouts  1.67 us (2%)
    pallas_call x1, Pallas kernels, per_device(): pl.pallas_call(functools.partial(kernel, ny, nx), out_shape=jax.ShapeDtyp...  67.3 us
    unnamed x1, local copies, waits for them, and re-layouts  1.67 us

profile of v1, /device:TPU:1, one launch (start us, length us, event | category | flops | bytes accessed | tf_op | source)
XLA Modules:
  0.0 69.0 jit_solution(2128455856363551679)
XLA Ops:
  0.0 67.3 %shard_map.37 = f32[16,32,128]{2,1,0:T(8,128)} custom-call(f32[16,32,128]{2,1,0:T(8,128)} %obs_hbm.1, f32[9,3,64]{2,1,0:T(4,128)} %bitcast.1, s32[16,32]{1,0:T(8,128)} %tiles.1), custom_call_target="tpu_custom_call" | custom-call | tf_op jit(solution)/shard_map/pallas_call | solution.py:540
  67.3 1.7 %copy.5 = f32[16,32,128]{2,1,0:T(8,128)} copy(f32[16,32,128]{2,1,0:T(8,128)} %shard_map.37) | data formatting | bytes 524288

commit v2 on v1

--- a/solution.py
+++ b/solution.py
@@ -25,11 +25,11 @@
     ny, nx,
     obs_hbm, prof, tiles, out_ref,
     u_ext, g_ext, grad, tv, resid, back, spread, blur_in, blur_y, flux,
-    fwd_hi, fwd_lo, bwd_hi, bwd_lo, lhs_hi, lhs_lo,
-    ux, gx_halo, own_edge, edge_pad, edge_spill,
+    fwd, bwd, bwd_lo, lhs_hi, lhs_lo,
+    ux, gx_halo, own_edge, edge_pad,
     send_y, recv_y, send_x, recv_x,
     part, all_x, part_y, all_y,
-    load_sem, send_sem, recv_sem, ar_send, ar_recv,
+    load_sem, send_sem, recv_sem, ar_send, ar_recv, known,
 ):
     row = lax.axis_index("gy")
     col = lax.axis_index("gx")
@@ -45,19 +45,8 @@
 
     barrier = pltpu.get_barrier_semaphore()
 
-    def greet_x(i, c):
-        pl.semaphore_signal(barrier, inc=1, device_id=at(0, i), device_id_type=MESH)
-        return c
-
-    def greet_y(i, c):
-        pl.semaphore_signal(barrier, inc=1, device_id=at(i, 0), device_id_type=MESH)
-        return c
-
-    lax.fori_loop(1, nx, greet_x, 0)
-    lax.fori_loop(1, ny, greet_y, 0)
-    for dy in (-1, 1):
-        for dx in (-1, 1):
-            pl.semaphore_signal(barrier, inc=1, device_id=at(dy, dx), device_id_type=MESH)
+    for dy, dx in SIDES:
+        pl.semaphore_signal(barrier, inc=1, device_id=at(dy, dx), device_id_type=MESH)
 
     number = tiles[row, col]
     depth = [prof[a, 0, number] for a in range(TAPS)]
@@ -72,46 +61,52 @@
     first_row, last_row = row == 0, row == ny - 1
     first_col, last_col = col == 0, col == nx - 1
 
-    mk = lax.broadcasted_iota(jnp.int32, (CX, CX), 0)
-    mn = lax.broadcasted_iota(jnp.int32, (CX, CX), 1)
-
-    def band(diff, offset):
-        total = jnp.zeros((CX, CX), F32)
-        for c in range(TAPS):
-            total = jnp.where(diff == c - offset, across[c], total)
-        return total
-
-    def wrapped(diff):
-        total = jnp.zeros((CX, CX), F32)
-        for c in range(TAPS):
-            hit = (diff == c - RADIUS - CX) | (diff == c - RADIUS + CX)
-            total = jnp.where(hit, across[c], total)
-        return total
+    load.wait()
 
     def halves(value):
         high = value.astype(BF16)
         return high, (value - high.astype(F32)).astype(BF16)
 
-    ahead = mn - mk
-    for part_no, w in enumerate((band(ahead, RADIUS), wrapped(ahead))):
-        high, low = halves(w)
-        fwd_hi[pl.ds(part_no * CX, CX), :] = high
-        fwd_lo[pl.ds(part_no * CX, CX), :] = low
-    behind = mk - mn
-    for part_no, w in enumerate((band(behind, RADIUS), wrapped(behind))):
-        high, low = halves(w)
-        bwd_hi[:, pl.ds(part_no * CX, CX)] = high
-        bwd_lo[:, pl.ds(part_no * CX, CX)] = low
-
-    back[:, pl.ds(0, 16), :] = jnp.zeros((Z, 16, CX), F32)
-    back[:, pl.ds(16 + CY, 16), :] = jnp.zeros((Z, 16, CX), F32)
-    edge_pad[pl.ds(0, 16), :] = jnp.zeros((16, CX), F32)
-    edge_pad[pl.ds(16 + CY, 16), :] = jnp.zeros((16, CX), F32)
-
-    load.wait()
-    pl.semaphore_wait(barrier, nx - 1 + ny - 1 + 4)
+    def prepare():
+        mk = lax.broadcasted_iota(jnp.int32, (CX, CX), 0)
+        mn = lax.broadcasted_iota(jnp.int32, (CX, CX), 1)
+
+        def band(diff, offset):
+            total = jnp.zeros((CX, CX), F32)
+            for c in range(TAPS):
+                total = jnp.where(diff == c - offset, across[c], total)
+            return total
+
+        def wrapped(diff):
+            total = jnp.zeros((CX, CX), F32)
+            for c in range(TAPS):
+                hit = (diff == c - RADIUS - CX) | (diff == c - RADIUS + CX)
+                total = jnp.where(hit, across[c], total)
+            return total
+
+        ahead = mn - mk
+        for part_no, w in enumerate((band(ahead, RADIUS), wrapped(ahead))):
+            high, low = halves(w)
+            fwd[pl.ds(part_no * CX, CX), pl.ds(0, CX)] = high
+            fwd[pl.ds(part_no * CX, CX), pl.ds(CX, CX)] = low
+        behind = mk - mn
+        for part_no, w in enumerate((band(behind, RADIUS), wrapped(behind))):
+            high, low = halves(w)
+            bwd[pl.ds(0, CX), pl.ds(part_no * CX, CX)] = high
+            bwd[pl.ds(CX, CX), pl.ds(part_no * CX, CX)] = high
+            bwd_lo[:, pl.ds(part_no * CX, CX)] = low
+
+        back[:, pl.ds(0, 16), :] = jnp.zeros((Z, 16, CX), F32)
+        back[:, pl.ds(16 + CY, 16), :] = jnp.zeros((Z, 16, CX), F32)
+        edge_pad[pl.ds(0, 16), :] = jnp.zeros((16, CX), F32)
+        edge_pad[pl.ds(16 + CY, 16), :] = jnp.zeros((16, CX), F32)
 
     def planes(body, init, step=4):
+        if step == Z:
+            for p in range(Z):
+                init = body(p, init)
+            return init
+
         def some(i, carry):
             for k in range(step):
                 carry = body(i * step + k, carry)
@@ -124,7 +119,7 @@
             turned = pltpu.roll(read(p), 8 * p + 4, 1)
             return jnp.where(plane_of == p, turned, total)
 
-        return planes(body, jnp.zeros((CY, CX), F32))
+        return planes(body, jnp.zeros((CY, CX), F32), Z)
 
     def copies(r):
         made = []
@@ -152,7 +147,7 @@
             made[k].start()
         return made
 
-    def halo_send(r, ext, edges_out):
+    def halo_stage(r, ext, edges_out):
         edge = pack_columns(lambda p: ext[p, pl.ds(8, CY), :])
         edges_out[...] = edge
         send_x[r, pl.ds(8, CY), :] = edge
@@ -163,7 +158,6 @@
             send_y[r, 0, q] = jnp.where(low_half, top, pltpu.roll(top2, 4, 0))
             low, low2 = ext[q, pl.ds(CY, 8), :], ext[q + 8, pl.ds(CY, 8), :]
             send_y[r, 1, q] = jnp.where(low_half, pltpu.roll(low, 4, 0), low2)
-        return send(r)
 
     def halo_wait(r, made, ext, halo):
         for c in made:
@@ -206,7 +200,7 @@
             total = along[0] * ext[p, pl.ds(8 + RADIUS, CY), :]
             for b in range(1, TAPS):
                 total = total + along[b] * ext[p, pl.ds(8 + RADIUS - b, CY), :]
-            here = pl.ds(pl.multiple_of(p * CY, CY), CY)
+            here = pl.ds(p * CY if isinstance(p, int) else pl.multiple_of(p * CY, CY), CY)
             high, low = halves(total)
             lhs_hi[here, pl.ds(0, CX)] = high
             lhs_lo[here, pl.ds(0, CX)] = low
@@ -216,37 +210,33 @@
             return c
 
         planes(body, 0)
-        mixed = jnp.dot(lhs_hi[...], fwd_hi[...], preferred_element_type=F32)
-        mixed = mixed + jnp.dot(lhs_lo[...], fwd_hi[...], preferred_element_type=F32)
-        mixed = mixed + jnp.dot(lhs_hi[...], fwd_lo[...], preferred_element_type=F32)
-        blur_y[:, pl.ds(0, CX)] = mixed
+        both = jnp.dot(lhs_hi[...], fwd[...], preferred_element_type=F32)
+        mixed = jnp.dot(lhs_lo[...], fwd[:, pl.ds(0, CX)], preferred_element_type=F32)
+        blur_y[:, pl.ds(0, CX)] = mixed + both[:, 0:CX] + both[:, CX : 2 * CX]
         depth_blur(lambda p, t: blur_y[pl.ds(p * CY + t * 8, 8), pl.ds(0, CX)], write, False)
 
     def spill_send(r, field):
         def keep(p, t, value):
             high, low = halves(value)
             here = pl.ds(p * CY + t * 8, 8)
-            blur_in[p, pl.ds(t * 8, 8), :] = value
+            lhs_hi[here, pl.ds(0, CX)] = high
+            lhs_hi[here, pl.ds(CX, CX)] = low
 
         depth_blur(lambda p, t: field[p, pl.ds(t * 8, 8), :], keep, True)
-        whole = blur_in[...].reshape(Z * CY, CX)
-        high, low = halves(whole)
-        mixed = jnp.dot(high, bwd_hi[...], preferred_element_type=F32)
-        mixed = mixed + jnp.dot(low, bwd_hi[...], preferred_element_type=F32)
-        mixed = mixed + jnp.dot(high, bwd_lo[...], preferred_element_type=F32)
+        mixed = jnp.dot(lhs_hi[...], bwd[...], preferred_element_type=F32)
+        mixed = mixed + jnp.dot(lhs_hi[:, pl.ds(0, CX)], bwd_lo[...], preferred_element_type=F32)
         blur_y[...] = mixed
 
         def split(p, total):
-            here = pl.ds(pl.multiple_of(p * CY, CY), CY)
+            here = pl.ds(p * CY if isinstance(p, int) else pl.multiple_of(p * CY, CY), CY)
             back[p, pl.ds(16, CY), :] = blur_y[here, pl.ds(0, CX)]
             turned = pltpu.roll(blur_y[here, pl.ds(CX, CX)], 8 * p + 4, 1)
             return jnp.where(plane_of == p, turned, total)
 
-        edge_pad[pl.ds(16, CY), :] = planes(split, jnp.zeros((CY, CX), F32))
+        edge_pad[pl.ds(16, CY), :] = planes(split, jnp.zeros((CY, CX), F32), Z)
         edge = along[0] * edge_pad[pl.ds(4, EXT), :]
         for b in range(1, TAPS):
             edge = edge + along[b] * edge_pad[pl.ds(4 + b, EXT), :]
-        edge_spill[...] = edge
         send_x[r] = edge
 
         def body(p, c):
@@ -312,7 +302,7 @@
             beyond = pltpu.roll(around, 124 - 8 * p, 1)
             dx = pltpu.roll(jnp.where(lane == 0, beyond, u), CX - 1, 1) - u
             dx = jnp.where(no_col_diff, 0.0, dx)
-            after = ext[jnp.minimum(p + 1, Z - 1), pl.ds(0, 40), :]
+            after = ext[min(p + 1, Z - 1) if isinstance(p, int) else jnp.minimum(p + 1, Z - 1), pl.ds(0, 40), :]
             dz = after - u
             inverse = inverse_size(dx, dy, dz)
             fy = jnp.where(no_row_flux, 0.0, dy * inverse)
@@ -325,7 +315,31 @@
             write(p, slope)
             return fz
 
-        planes(body, jnp.zeros((CY, CX), F32), 2)
+        planes(body, jnp.zeros((CY, CX), F32), 4)
+
+    def rows8(value):
+        return value[0:8] + value[8:16] + value[16:24] + value[24:32]
+
+    def variation_dot(ext, halo, other, other_halo):
+        around, other_around = halo[pl.ds(8, CY), :], other_halo[pl.ds(8, CY), :]
+        final_row = last_row & (rows32 == CY - 1)
+
+        def shifted(u, side, p):
+            beyond = pltpu.roll(side, 124 - 8 * p, 1)
+            return pltpu.roll(jnp.where(lane == 0, beyond, u), CX - 1, 1) - u
+
+        def body(p, total):
+            u, g = ext[p, pl.ds(8, CY), :], other[p, pl.ds(8, CY), :]
+            after = min(p + 1, Z - 1) if isinstance(p, int) else jnp.minimum(p + 1, Z - 1)
+            dz = ext[after, pl.ds(8, CY), :] - u
+            ez = other[after, pl.ds(8, CY), :] - g
+            dy = jnp.where(final_row, 0.0, ext[p, pl.ds(9, CY), :] - u)
+            ey = other[p, pl.ds(9, CY), :] - g
+            dx = jnp.where(no_col_diff, 0.0, shifted(u, around, p))
+            ex = shifted(g, other_around, p)
+            return total + rows8((dx * ex + dy * ey + dz * ez) * inverse_size(dx, dy, dz))
+
+        return planes(body, jnp.zeros((8, CX), F32), 4)
 
     def fold(values):
         total = jnp.zeros((1, CX), F32)
@@ -336,20 +350,29 @@
             total = jnp.where(lane // 32 == i, v, total)
         return total
 
+    def far_first_x():
+        if nx != 32:
+            return [lax.rem(col + i, nx) for i in range(1, nx)]
+        x, y, core = col // 8, lax.rem(col // 2, 4), lax.rem(col, 2)
+        xs = [lax.rem(x + i, 4) * 8 for i in range(4)]
+        ys = [lax.rem(y + i, 4) * 2 for i in range(4)]
+        cores = [core, 1 - core]
+        ring = (0, 1, 2, 1)
+        moves = [(i, j, k) for i in range(4) for j in range(4) for k in range(2)][1:]
+        moves.sort(key=lambda m: -(ring[m[0]] + ring[m[1]] + 0.3 * m[2]))
+        return [xs[i] + ys[j] + cores[k] for i, j, k in moves]
+
     def reduce_start(a, values):
         mine = fold(values)
         part[a] = mine
         all_x[a, pl.ds(col, 1)] = mine.reshape(1, 1, CX)
 
-        def go(i, c):
+        for peer in far_first_x():
             pltpu.make_async_remote_copy(
                 src_ref=part.at[a], dst_ref=all_x.at[a, col],
                 send_sem=ar_send.at[a, 0], recv_sem=ar_recv.at[a, 0],
-                device_id=at(0, i), device_id_type=MESH,
+                device_id={"gy": row, "gx": peer}, device_id_type=MESH,
             ).start()
-            return c
-
-        lax.fori_loop(1, nx, go, 0)
 
     def reduce_middle(a):
         got = all_x.at[a, pl.ds(0, nx - 1)]
@@ -358,15 +381,12 @@
         part_y[a] = mine
         all_y[a, pl.ds(row, 1)] = mine.reshape(1, 1, CX)
 
-        def go(i, c):
+        for i in sorted(range(1, ny), key=lambda i: -min(i, ny - i)):
             pltpu.make_async_remote_copy(
                 src_ref=part_y.at[a], dst_ref=all_y.at[a, row],
                 send_sem=ar_send.at[a, 1], recv_sem=ar_recv.at[a, 1],
                 device_id=at(i, 0), device_id_type=MESH,
             ).start()
-            return c
-
-        lax.fori_loop(1, ny, go, 0)
 
     def reduce_end(a):
         got = all_y.at[a, pl.ds(0, ny - 1)]
@@ -374,30 +394,29 @@
         total = jnp.sum(all_y[a], axis=0)
         return [jnp.sum(jnp.where(lane // 32 == i, total, 0.0), axis=1, keepdims=True) for i in range(3)]
 
-    def rows8(value):
-        return value[0:8] + value[8:16] + value[16:24] + value[24:32]
-
     zero8 = jnp.zeros((8, CX), F32)
     main = pl.ds(8, CY)
 
-    waiting = []
-    made = halo_send(0, u_ext, own_edge.at[0])
-    waiting += made
-    halo_wait(0, made, u_ext, ux)
+    def tell(level, distance):
+        for axis, n in enumerate((ny, nx)):
+            if n // 2 > distance:
+                for d in (-distance, distance):
+                    pl.semaphore_signal(
+                        known.at[axis, level], inc=1,
+                        device_id=at(d, 0) if axis == 0 else at(0, d), device_id_type=MESH,
+                    )
+
+    def hear(level, distance):
+        for axis, n in enumerate((ny, nx)):
+            if n // 2 > distance:
+                pl.semaphore_wait(known.at[axis, level], 2)
 
     def keep_residual(p, t, value):
         here = pl.ds(t * 8, 8)
         resid[p, here, :] = value - u_ext[p, pl.ds(8 + t * 8, 8), :]
 
-    blur(u_ext, ux, keep_residual)
-    made = spill_send(1, resid)
-    waiting += made
-
     def keep_tv(p, slope):
         tv[p] = slope
-
-    variation(u_ext, ux, own_edge[0], keep_tv)
-    spill_wait(1, made)
 
     def gradient(target):
         def body(p, c):
@@ -408,11 +427,6 @@
 
         planes(body, 0)
 
-    gradient(g_ext)
-    made = halo_send(2, g_ext, own_edge.at[1])
-    waiting += made
-    halo_wait(2, made, g_ext, gx_halo)
-
     def advance(step):
         def body(p, c):
             u_ext[p] = u_ext[p] - step * g_ext[p]
@@ -432,28 +446,38 @@
         def body(p, c):
             g = g_ext[p, main, :]
             h = grad[p]
-            return c[0] + rows8(g * g), c[1] + rows8(h * h)
-
-        return planes(body, (zero8, zero8))
-
-    def variation_change():
-        def keep(p, slope):
-            blur_in[p] = slope
-
-        variation(u_ext, ux, own_edge[0], keep)
-
-        def body(p, c):
-            new = blur_in[p]
-            c = c + rows8(g_ext[p, main, :] * (new - tv[p]))
-            tv[p] = new
-            return c
-
-        return planes(body, zero8)
+            return c[0] + rows8(g * g), c[1] + rows8(h * h), c[2] + rows8(g * tv[p])
+
+        return planes(body, (zero8, zero8, zero8))
+
+    waiting = []
+    halo_stage(0, u_ext, own_edge.at[0])
+    pl.semaphore_wait(barrier, len(SIDES))
+    made = send(0)
+    waiting += made
+    prepare()
+    halo_wait(0, made, u_ext, ux)
+    tell(0, 2)
+    blur(u_ext, ux, keep_residual)
+    made = spill_send(1, resid)
+    waiting += made
+    variation(u_ext, ux, own_edge[0], keep_tv)
+    spill_wait(1, made)
+    hear(0, 2)
+    tell(1, 4)
+    gradient(g_ext)
+    halo_stage(2, g_ext, own_edge.at[1])
+    made = send(2)
+    waiting += made
+    halo_wait(2, made, g_ext, gx_halo)
+    hear(1, 4)
+    tell(2, 8)
 
     advance(START_STEP)
     blur_gradient()
-    gg, hh = sums_of_gradient()
-    gt = variation_change()
+    gg, hh, gt = sums_of_gradient()
+    gt = variation_dot(u_ext, ux, g_ext, gx_halo) - gt
+    hear(2, 8)
     reduce_start(0, (gg, hh, gt))
 
     def body(p, c):
@@ -463,29 +487,35 @@
     planes(body, 0)
     made = spill_send(3, resid)
     waiting += made
+    variation(u_ext, ux, own_edge[0], keep_tv)
     reduce_middle(0)
     spill_wait(3, made)
     gradient(g_ext)
+    halo_stage(4, g_ext, own_edge.at[1])
+    made = send(4)
+    waiting += made
+
     def keep_spread(p, c):
         resid[p] = spread[p, main, :]
         return c
 
     planes(keep_spread, 0)
-    made = halo_send(4, g_ext, own_edge.at[1])
-    waiting += made
     halo_wait(4, made, g_ext, gx_halo)
     blur_gradient()
-    gg, hh = sums_of_gradient()
-    made = spill_send(5, grad)
-    waiting += made
+    gg, hh, gt = sums_of_gradient()
     g2, h2, t2 = reduce_end(0)
     change_sq = START_STEP * START_STEP * g2
     change_growth = START_STEP * START_STEP * (h2 + DAMPING * g2) - START_STEP * WEIGHT_TV * t2
     step = change_sq / change_growth
 
     advance(step)
-    gt = variation_change()
+    gt = variation_dot(u_ext, ux, g_ext, gx_halo) - gt
     reduce_start(1, (gg, hh, gt))
+
+    made = spill_send(5, grad)
+    waiting += made
+    variation(u_ext, ux, own_edge[0], keep_tv)
+    reduce_middle(1)
     spill_wait(5, made)
 
     def last(p, c):
@@ -493,7 +523,6 @@
         g_ext[p, main, :] = pulled + WEIGHT_TV * tv[p] + DAMPING * u_ext[p, main, :]
         return c
 
-    reduce_middle(1)
     planes(last, 0)
     g2, h2, t2 = reduce_end(1)
     change_sq = step * step * g2
@@ -523,12 +552,11 @@
         extended, extended, field, field, field,
         pltpu.VMEM((Z, CY + 32, CX), F32), extended, field,
         pltpu.VMEM((Z * CY, 2 * CX), F32), pltpu.VMEM((40, CX), F32),
-        pltpu.VMEM((2 * CX, CX), BF16), pltpu.VMEM((2 * CX, CX), BF16),
-        pltpu.VMEM((CX, 2 * CX), BF16), pltpu.VMEM((CX, 2 * CX), BF16),
+        pltpu.VMEM((2 * CX, 2 * CX), BF16), pltpu.VMEM((2 * CX, 2 * CX), BF16),
+        pltpu.VMEM((CX, 2 * CX), BF16),
         pltpu.VMEM((Z * CY, 2 * CX), BF16), pltpu.VMEM((Z * CY, 2 * CX), BF16),
         pltpu.VMEM((EXT, CX), F32), pltpu.VMEM((EXT, CX), F32),
         pltpu.VMEM((2, CY, CX), F32), pltpu.VMEM((CY + 32, CX), F32),
-        pltpu.VMEM((EXT, CX), F32),
         pltpu.VMEM((rounds, 2, 8, 8, CX), F32), pltpu.VMEM((rounds, 2, 8, 8, CX), F32),
         pltpu.VMEM((rounds, EXT, CX), F32), pltpu.VMEM((rounds, 2, EXT, CX), F32),
         pltpu.VMEM((2, 1, CX), F32), pltpu.VMEM((2, nx, 1, CX), F32),
@@ -536,6 +564,7 @@
         pltpu.SemaphoreType.DMA,
         pltpu.SemaphoreType.DMA((rounds, 8)), pltpu.SemaphoreType.DMA((rounds, 8)),
         pltpu.SemaphoreType.DMA((2, 2)), pltpu.SemaphoreType.DMA((2, 2)),
+        pltpu.SemaphoreType.REGULAR((2, 3)),
     ]
     return pl.pallas_call(
         functools.partial(kernel, ny, nx),

time: 69.3 us -> 63 us (0.909)
  Pallas kernels: 67.3 us -> 61.1 us
    pallas_call x1, Pallas kernels: 67.3 us -> 61.1 us  [per_device(): pl.pallas_call(functools.partial(kernel, ny, nx), out_shape=jax.ShapeDtyp...]
where the time goes in v2:
time: 63 us; the launch traced here: 62.8 us
  Pallas kernels  61.1 us (97%)
  local copies, waits for them, and re-layouts  1.67 us (3%)
    pallas_call x1, Pallas kernels, per_device(): pl.pallas_call(functools.partial(kernel, ny, nx), out_shape=jax.ShapeDtyp...  61.1 us
    unnamed x1, local copies, waits for them, and re-layouts  1.67 us

profile of v2, /device:TPU:1, one launch (start us, length us, event | category | flops | bytes accessed | tf_op | source)
XLA Modules:
  0.0 62.8 jit_solution(15728159385860123857)
XLA Ops:
  0.0 61.1 %shard_map.37 = f32[16,32,128]{2,1,0:T(8,128)} custom-call(f32[16,32,128]{2,1,0:T(8,128)} %obs_hbm.1, f32[9,3,64]{2,1,0:T(4,128)} %bitcast.1, s32[16,32]{1,0:T(8,128)} %tiles.1), custom_call_target="tpu_custom_call" | custom-call | tf_op jit(solution)/shard_map/pallas_call | solution.py:569
  61.1 1.7 %copy.5 = f32[16,32,128]{2,1,0:T(8,128)} copy(f32[16,32,128]{2,1,0:T(8,128)} %shard_map.37) | data formatting | bytes 524288

commit v3 on v2

--- a/solution.py
+++ b/solution.py
@@ -24,8 +24,8 @@
 def kernel(
     ny, nx,
     obs_hbm, prof, tiles, out_ref,
-    u_ext, g_ext, grad, tv, resid, back, spread, blur_in, blur_y, flux,
-    fwd, bwd, bwd_lo, lhs_hi, lhs_lo,
+    u_ext, g_ext, grad, tv, resid, back, spread, blur_y, flux,
+    fwd, bwd, side_fwd, side_bwd, twice, y_fix, x_fix,
     ux, gx_halo, own_edge, edge_pad,
     send_y, recv_y, send_x, recv_x,
     part, all_x, part_y, all_y,
@@ -61,6 +61,10 @@
     first_row, last_row = row == 0, row == ny - 1
     first_col, last_col = col == 0, col == nx - 1
 
+    back[:, pl.ds(0, 16), :] = jnp.zeros((Z, 16, CX), F32)
+    back[:, pl.ds(16 + CY, 16), :] = jnp.zeros((Z, 16, CX), F32)
+    edge_pad[pl.ds(0, 16), :] = jnp.zeros((16, CX), F32)
+    edge_pad[pl.ds(16 + CY, 16), :] = jnp.zeros((16, CX), F32)
     load.wait()
 
     def halves(value):
@@ -71,35 +75,34 @@
         mk = lax.broadcasted_iota(jnp.int32, (CX, CX), 0)
         mn = lax.broadcasted_iota(jnp.int32, (CX, CX), 1)
 
-        def band(diff, offset):
+        def band(diff, taps, keep=None):
             total = jnp.zeros((CX, CX), F32)
             for c in range(TAPS):
-                total = jnp.where(diff == c - offset, across[c], total)
-            return total
-
-        def wrapped(diff):
-            total = jnp.zeros((CX, CX), F32)
-            for c in range(TAPS):
-                hit = (diff == c - RADIUS - CX) | (diff == c - RADIUS + CX)
-                total = jnp.where(hit, across[c], total)
-            return total
+                total = jnp.where(diff == c - RADIUS, taps[c], total)
+            return total if keep is None else jnp.where(keep, total, 0.0)
 
         ahead = mn - mk
-        for part_no, w in enumerate((band(ahead, RADIUS), wrapped(ahead))):
-            high, low = halves(w)
-            fwd[pl.ds(part_no * CX, CX), pl.ds(0, CX)] = high
-            fwd[pl.ds(part_no * CX, CX), pl.ds(CX, CX)] = low
-        behind = mk - mn
-        for part_no, w in enumerate((band(behind, RADIUS), wrapped(behind))):
-            high, low = halves(w)
-            bwd[pl.ds(0, CX), pl.ds(part_no * CX, CX)] = high
-            bwd[pl.ds(CX, CX), pl.ds(part_no * CX, CX)] = high
-            bwd_lo[:, pl.ds(part_no * CX, CX)] = low
-
-        back[:, pl.ds(0, 16), :] = jnp.zeros((Z, 16, CX), F32)
-        back[:, pl.ds(16 + CY, 16), :] = jnp.zeros((Z, 16, CX), F32)
-        edge_pad[pl.ds(0, 16), :] = jnp.zeros((16, CX), F32)
-        edge_pad[pl.ds(16 + CY, 16), :] = jnp.zeros((16, CX), F32)
+        planes_ahead = mn // 8 - mk // 8
+        places_ahead = ahead - 8 * planes_ahead
+        crossing = (mn // 4 + mk // 4) % 2 == 1
+        for ref, sign in ((fwd, 1), (bwd, -1)):
+            split_matrix(ref, band(sign * ahead, across))
+        for ref, sign in ((side_fwd, 1), (side_bwd, -1)):
+            split_matrix(
+                ref, band(sign * planes_ahead, depth) * band(sign * places_ahead, across, crossing)
+            )
+
+    def split_matrix(ref, w):
+        high, low = halves(w)
+        ref[pl.ds(0, CX), pl.ds(0, CX)] = high
+        ref[pl.ds(CX, CX), pl.ds(0, CX)] = high
+        ref[pl.ds(0, CX), pl.ds(CX, CX)] = low
+        ref[pl.ds(CX, CX), pl.ds(CX, CX)] = jnp.zeros((CX, CX), BF16)
+
+    def times(value, ref):
+        high, low = halves(value)
+        both = jnp.dot(jnp.concatenate([high, low], axis=1), ref[...], preferred_element_type=F32)
+        return both[:, 0:CX] + both[:, CX : 2 * CX]
 
     def planes(body, init, step=4):
         if step == Z:
@@ -147,29 +150,107 @@
             made[k].start()
         return made
 
-    def halo_stage(r, ext, edges_out):
-        edge = pack_columns(lambda p: ext[p, pl.ds(8, CY), :])
-        edges_out[...] = edge
+    border = (lane < 4) | (lane >= CX - 4)
+
+    def mixing(taps):
+        limits = {1: (sub8 <= 0, 5), 2: (sub8 <= 1, 6), 3: (sub8 <= 2, 7), 5: (sub8 >= 5, 1), 6: (sub8 >= 6, 2), 7: (sub8 >= 7, 3)}
+        weights = {s: jnp.where(mask, taps[b], 0.0) for s, (mask, b) in limits.items()}
+        weights[4] = jnp.where(low_half, taps[8], taps[0])
+        return weights
+
+    def put_rows(rows, first, second):
+        for q in range(8):
+            a, b = rows[q], pltpu.roll(rows[q + 8], 4, 0)
+            first[q] = jnp.where(low_half, a, b)
+            second[q] = jnp.where(low_half, b, a)
+
+    def get_rows(first, second, no_first, no_second):
+        near, far = [], []
+        for q in range(8):
+            a = jnp.where(no_first, 0.0, first[q])
+            b = jnp.where(no_second, 0.0, second[q])
+            near.append(jnp.where(low_half, a, b))
+            far.append(pltpu.roll(jnp.where(low_half, b, a), 4, 0))
+        return near + far
+
+    def cross(rows, taps, transposed, ref):
+        for p in range(Z):
+            twice[p, pl.ds(0, 8), :] = rows[p]
+            twice[p, pl.ds(8, 8), :] = rows[p]
+        weights = mixing(taps)
+        mixed = []
+        for p in range(Z):
+            total = weights[4] * twice[p, pl.ds(4, 8), :]
+            for s in (1, 2, 3, 5, 6, 7):
+                total = total + weights[s] * twice[p, pl.ds(8 - s, 8), :]
+            mixed.append(total)
+        return times(jnp.concatenate(depth_sum(mixed, transposed), axis=0), ref)
+
+    def edge_rows(read):
+        return [jnp.where(low_half, read(p, 0), read(p, CY - 8)) for p in range(Z)]
+
+    def halo_send(r, rows, edge):
+        put_rows(rows, send_y.at[r, 0], send_y.at[r, 1])
         send_x[r, pl.ds(8, CY), :] = edge
         send_x[r, pl.ds(0, 8), :] = edge[0:8]
         send_x[r, pl.ds(8 + CY, 8), :] = edge[CY - 8 : CY]
-        for q in range(8):
-            top, top2 = ext[q, pl.ds(8, 8), :], ext[q + 8, pl.ds(8, 8), :]
-            send_y[r, 0, q] = jnp.where(low_half, top, pltpu.roll(top2, 4, 0))
-            low, low2 = ext[q, pl.ds(CY, 8), :], ext[q + 8, pl.ds(CY, 8), :]
-            send_y[r, 1, q] = jnp.where(low_half, pltpu.roll(low, 4, 0), low2)
-
-    def halo_wait(r, made, ext, halo):
+        return send(r)
+
+    def halo_fix(r, made, ext, halo):
         for c in made:
             c.wait_recv()
-        for q in range(8):
-            above = jnp.where(first_row, 0.0, recv_y[r, 0, q])
-            ext[q, pl.ds(0, 8), :] = pltpu.roll(above, 4, 0)
-            ext[q + 8, pl.ds(0, 8), :] = above
-            below = jnp.where(last_row, 0.0, recv_y[r, 1, q])
-            ext[q, pl.ds(8 + CY, 8), :] = below
-            ext[q + 8, pl.ds(8 + CY, 8), :] = pltpu.roll(below, 4, 0)
+        rows = get_rows(recv_y.at[r, 1], recv_y.at[r, 0], last_row, first_row)
+        for p in range(Z):
+            ext[p, pl.ds(0, 8), :] = rows[p]
+            ext[p, pl.ds(8 + CY, 8), :] = rows[p]
         halo[...] = sides(r, place < 4)
+        edge = along[0] * halo[pl.ds(8 + RADIUS, CY), :]
+        for b in range(1, TAPS):
+            edge = edge + along[b] * halo[pl.ds(8 + RADIUS - b, CY), :]
+        x_fix[...] = times(edge, side_fwd)
+        y_fix[...] = cross(rows, along, False, fwd)
+
+    def spill_send(r, rows, edge):
+        edge_pad[pl.ds(16, CY), :] = times(edge, side_bwd)
+        spilled = cross(rows, along[::-1], True, bwd)
+        put_rows([spilled[8 * p : 8 * p + 8] for p in range(Z)], send_y.at[r, 1], send_y.at[r, 0])
+        total = along[0] * edge_pad[pl.ds(4, EXT), :]
+        for b in range(1, TAPS):
+            total = total + along[b] * edge_pad[pl.ds(4 + b, EXT), :]
+        send_x[r] = total
+        return send(r)
+
+    def spill_fix(r, made):
+        for c in made:
+            c.wait_recv()
+        rows = get_rows(recv_y.at[r, 0], recv_y.at[r, 1], first_row, last_row)
+        y_fix[...] = jnp.concatenate(rows, axis=0)
+        both = sides(r, place >= 4)
+        x_fix[pl.ds(0, 8), :] = both[8:16] + both[0:8]
+        x_fix[pl.ds(8, 16), :] = both[16:CY]
+        x_fix[pl.ds(24, 8), :] = both[CY : CY + 8] + both[CY + 8 : CY + 16]
+
+    def fixed_edges(read, edge):
+        extra = x_fix[...]
+        ends = jnp.where(low_half, extra[0:8], extra[CY - 8 : CY])
+        rows, packed = edge_rows(read), jnp.zeros((8, CX), F32)
+        for p in range(Z):
+            y = y_fix[pl.ds(8 * p, 8), :]
+            packed = jnp.where(plane_of == p, pltpu.roll(y, 8 * p + 4, 1), packed)
+            rows[p] = rows[p] + y + jnp.where(border, pltpu.roll(ends, 124 - 8 * p, 1), 0.0)
+        edge = edge + extra
+        top = edge[0:8] + jnp.where(low_half, packed, 0.0)
+        low = edge[CY - 8 : CY] + jnp.where(low_half, 0.0, packed)
+        return rows, jnp.concatenate([top, edge[8 : CY - 8], low], axis=0)
+
+    def with_fix(add):
+        extra = x_fix[...]
+        for p in range(Z):
+            e = jnp.where(border, pltpu.roll(extra, 124 - 8 * p, 1), 0.0)
+            y = y_fix[pl.ds(8 * p, 8), :]
+            top = e[0:8] + jnp.where(low_half, y, 0.0)
+            low = e[CY - 8 : CY] + jnp.where(low_half, 0.0, y)
+            add(p, jnp.concatenate([top, e[8 : CY - 8], low], axis=0))
 
     def sides(r, from_left):
         left = jnp.where(first_col, 0.0, recv_x[r, 0])
@@ -179,104 +260,49 @@
         both = jnp.where(first_row & (at_row < 8), 0.0, both)
         return jnp.where(last_row & (at_row >= 8 + CY), 0.0, both)
 
-    def depth_blur(read, write, transposed):
+    def depth_sum(value, transposed):
+        out = []
+        for p in range(Z):
+            total = None
+            for a in range(TAPS):
+                source = p - RADIUS + a if transposed else p + RADIUS - a
+                if 0 <= source < Z:
+                    term = depth[a] * value[source]
+                    total = term if total is None else total + term
+            out.append(total)
+        return out
+
+    def clear_border(ext):
+        for p in range(Z):
+            ext[p, pl.ds(0, 8), :] = jnp.zeros((8, CX), F32)
+            ext[p, pl.ds(8 + CY, 8), :] = jnp.zeros((8, CX), F32)
+
+    def blur_inside(ext, write):
+        for group in range(4):
+            rows = []
+            for p in range(4 * group, 4 * group + 4):
+                total = along[0] * ext[p, pl.ds(8 + RADIUS, CY), :]
+                for b in range(1, TAPS):
+                    total = total + along[b] * ext[p, pl.ds(8 + RADIUS - b, CY), :]
+                rows.append(total)
+            blur_y[pl.ds(group * 128, 128), :] = times(jnp.concatenate(rows, axis=0), fwd)
         for t in range(CY // 8):
-            value = [read(p, t) for p in range(Z)]
+            value = [blur_y[pl.ds(p * CY + t * 8, 8), :] for p in range(Z)]
+            for p, total in enumerate(depth_sum(value, False)):
+                write(p, t, total)
+
+    def spread_inside(field, write):
+        for t in range(CY // 8):
+            value = [field[p, pl.ds(t * 8, 8), :] for p in range(Z)]
+            out = times(jnp.concatenate(depth_sum(value, True), axis=0), bwd)
             for p in range(Z):
-                total = None
-                for a in range(TAPS):
-                    source = p - RADIUS + a if transposed else p + RADIUS - a
-                    if 0 <= source < Z:
-                        term = depth[a] * value[source]
-                        total = term if total is None else total + term
-                write(p, t, total)
-
-    def blur(ext, halo, write):
-        edge = jnp.zeros((CY, CX), F32)
-        for b in range(TAPS):
-            edge = edge + along[b] * halo[pl.ds(8 + RADIUS - b, CY), :]
-
-        def body(p, c):
-            total = along[0] * ext[p, pl.ds(8 + RADIUS, CY), :]
+                back[p, pl.ds(16 + t * 8, 8), :] = out[8 * p : 8 * p + 8]
+
+        for p in range(Z):
+            total = along[0] * back[p, pl.ds(12, CY), :]
             for b in range(1, TAPS):
-                total = total + along[b] * ext[p, pl.ds(8 + RADIUS - b, CY), :]
-            here = pl.ds(p * CY if isinstance(p, int) else pl.multiple_of(p * CY, CY), CY)
-            high, low = halves(total)
-            lhs_hi[here, pl.ds(0, CX)] = high
-            lhs_lo[here, pl.ds(0, CX)] = low
-            high, low = halves(pltpu.roll(edge, 124 - 8 * p, 1))
-            lhs_hi[here, pl.ds(CX, CX)] = high
-            lhs_lo[here, pl.ds(CX, CX)] = low
-            return c
-
-        planes(body, 0)
-        both = jnp.dot(lhs_hi[...], fwd[...], preferred_element_type=F32)
-        mixed = jnp.dot(lhs_lo[...], fwd[:, pl.ds(0, CX)], preferred_element_type=F32)
-        blur_y[:, pl.ds(0, CX)] = mixed + both[:, 0:CX] + both[:, CX : 2 * CX]
-        depth_blur(lambda p, t: blur_y[pl.ds(p * CY + t * 8, 8), pl.ds(0, CX)], write, False)
-
-    def spill_send(r, field):
-        def keep(p, t, value):
-            high, low = halves(value)
-            here = pl.ds(p * CY + t * 8, 8)
-            lhs_hi[here, pl.ds(0, CX)] = high
-            lhs_hi[here, pl.ds(CX, CX)] = low
-
-        depth_blur(lambda p, t: field[p, pl.ds(t * 8, 8), :], keep, True)
-        mixed = jnp.dot(lhs_hi[...], bwd[...], preferred_element_type=F32)
-        mixed = mixed + jnp.dot(lhs_hi[:, pl.ds(0, CX)], bwd_lo[...], preferred_element_type=F32)
-        blur_y[...] = mixed
-
-        def split(p, total):
-            here = pl.ds(p * CY if isinstance(p, int) else pl.multiple_of(p * CY, CY), CY)
-            back[p, pl.ds(16, CY), :] = blur_y[here, pl.ds(0, CX)]
-            turned = pltpu.roll(blur_y[here, pl.ds(CX, CX)], 8 * p + 4, 1)
-            return jnp.where(plane_of == p, turned, total)
-
-        edge_pad[pl.ds(16, CY), :] = planes(split, jnp.zeros((CY, CX), F32), Z)
-        edge = along[0] * edge_pad[pl.ds(4, EXT), :]
-        for b in range(1, TAPS):
-            edge = edge + along[b] * edge_pad[pl.ds(4 + b, EXT), :]
-        send_x[r] = edge
-
-        def body(p, c):
-            total = along[0] * back[p, pl.ds(4, EXT), :]
-            for b in range(1, TAPS):
-                total = total + along[b] * back[p, pl.ds(4 + b, EXT), :]
-            spread[p] = total
-            return c
-
-        planes(body, 0)
-        for q in range(8):
-            top, top2 = spread[q, pl.ds(0, 8), :], spread[q + 8, pl.ds(0, 8), :]
-            send_y[r, 0, q] = jnp.where(low_half, pltpu.roll(top, 4, 0), top2)
-            low, low2 = spread[q, pl.ds(8 + CY, 8), :], spread[q + 8, pl.ds(8 + CY, 8), :]
-            send_y[r, 1, q] = jnp.where(low_half, low, pltpu.roll(low2, 4, 0))
-        return send(r)
-
-    def spill_wait(r, made):
-        for c in made:
-            c.wait_recv()
-        both = sides(r, place >= 4)
-        top = both[8:16] + both[0:8]
-        low = both[CY : CY + 8] + both[CY + 8 : CY + 16]
-        edge = jnp.concatenate([top, both[16:CY], low], axis=0)
-        border = (lane < 4) | (lane >= CX - 4)
-        for q in range(8):
-            above = jnp.where(first_row, 0.0, recv_y[r, 0, q])
-            below = jnp.where(last_row, 0.0, recv_y[r, 1, q])
-            t, b = pl.ds(8, 8), pl.ds(CY, 8)
-            spread[q, t, :] = spread[q, t, :] + jnp.where(low_half, above, 0.0)
-            spread[q + 8, t, :] = spread[q + 8, t, :] + jnp.where(low_half, pltpu.roll(above, 4, 0), 0.0)
-            spread[q, b, :] = spread[q, b, :] + jnp.where(low_half, 0.0, pltpu.roll(below, 4, 0))
-            spread[q + 8, b, :] = spread[q + 8, b, :] + jnp.where(low_half, 0.0, below)
-
-        def body(p, c):
-            extra = jnp.where(border, pltpu.roll(edge, 124 - 8 * p, 1), 0.0)
-            spread[p, pl.ds(8, CY), :] = spread[p, pl.ds(8, CY), :] + extra
-            return c
-
-        planes(body, 0)
+                total = total + along[b] * back[p, pl.ds(12 + b, CY), :]
+            write(p, total)
 
     rows40 = lax.broadcasted_iota(jnp.int32, (40, CX), 0)
     rows32 = lax.broadcasted_iota(jnp.int32, (CY, CX), 0)
@@ -411,21 +437,8 @@
             if n // 2 > distance:
                 pl.semaphore_wait(known.at[axis, level], 2)
 
-    def keep_residual(p, t, value):
-        here = pl.ds(t * 8, 8)
-        resid[p, here, :] = value - u_ext[p, pl.ds(8 + t * 8, 8), :]
-
     def keep_tv(p, slope):
         tv[p] = slope
-
-    def gradient(target):
-        def body(p, c):
-            target[p, main, :] = (
-                spread[p, main, :] + WEIGHT_TV * tv[p] + DAMPING * u_ext[p, main, :]
-            )
-            return c
-
-        planes(body, 0)
 
     def advance(step):
         def body(p, c):
@@ -436,11 +449,45 @@
         ux[...] = ux[...] - step * gx_halo[...]
         own_edge[0] = own_edge[0] - step * own_edge[1]
 
-    def blur_gradient():
-        def keep(p, t, value):
-            grad[p, pl.ds(t * 8, 8), :] = value
-
-        blur(g_ext, gx_halo, keep)
+    def read_main(ext):
+        return lambda p, start: ext[p, pl.ds(8 + start, 8), :]
+
+    def read_field(field):
+        return lambda p, start: field[p, pl.ds(start, 8), :]
+
+    def packed_main(ext):
+        return pack_columns(lambda p: ext[p, main, :])
+
+    def add_main(p, extra):
+        g_ext[p, main, :] = g_ext[p, main, :] + extra
+
+    def add_grad(p, extra):
+        grad[p] = grad[p] + extra
+
+    def add_resid(p, extra):
+        resid[p] = resid[p] + extra
+
+    def keep_grad(p, t, value):
+        grad[p, pl.ds(t * 8, 8), :] = value
+
+    def keep_spread(p, value):
+        spread[p] = value
+
+    def gradient_inside():
+        def body(p, c):
+            g_ext[p, main, :] = spread[p] + WEIGHT_TV * tv[p] + DAMPING * u_ext[p, main, :]
+            return c
+
+        planes(body, 0)
+
+    def send_gradient(r, edge):
+        rows, edge = fixed_edges(read_main(g_ext), edge)
+        own_edge[1] = edge
+        return halo_send(r, rows, edge)
+
+    def spread_and_slope(field):
+        spread_inside(field, keep_spread)
+        variation(u_ext, ux, own_edge[0], keep_tv)
 
     def sums_of_gradient():
         def body(p, c):
@@ -451,57 +498,72 @@
         return planes(body, (zero8, zero8, zero8))
 
     waiting = []
-    halo_stage(0, u_ext, own_edge.at[0])
+    clear_border(u_ext)
+    edge = packed_main(u_ext)
+    own_edge[0] = edge
+    rows = edge_rows(read_main(u_ext))
     pl.semaphore_wait(barrier, len(SIDES))
-    made = send(0)
+    made = halo_send(0, rows, edge)
     waiting += made
     prepare()
-    halo_wait(0, made, u_ext, ux)
+
+    def keep_residual(p, t, value):
+        resid[p, pl.ds(t * 8, 8), :] = value - u_ext[p, pl.ds(8 + t * 8, 8), :]
+
+    blur_inside(u_ext, keep_residual)
+    edge = pack_columns(lambda p: resid[p])
+    halo_fix(0, made, u_ext, ux)
+    rows, edge = fixed_edges(read_field(resid), edge)
+    made = spill_send(1, rows, edge)
+    waiting += made
     tell(0, 2)
-    blur(u_ext, ux, keep_residual)
-    made = spill_send(1, resid)
+    with_fix(add_resid)
+    spread_and_slope(resid)
+    gradient_inside()
+    edge = packed_main(g_ext)
+    spill_fix(1, made)
+    made = send_gradient(2, edge)
     waiting += made
-    variation(u_ext, ux, own_edge[0], keep_tv)
-    spill_wait(1, made)
     hear(0, 2)
     tell(1, 4)
-    gradient(g_ext)
-    halo_stage(2, g_ext, own_edge.at[1])
-    made = send(2)
-    waiting += made
-    halo_wait(2, made, g_ext, gx_halo)
+    with_fix(add_main)
+    clear_border(g_ext)
+    blur_inside(g_ext, keep_grad)
+    halo_fix(2, made, g_ext, gx_halo)
     hear(1, 4)
     tell(2, 8)
+    with_fix(add_grad)
 
     advance(START_STEP)
-    blur_gradient()
     gg, hh, gt = sums_of_gradient()
     gt = variation_dot(u_ext, ux, g_ext, gx_halo) - gt
     hear(2, 8)
     reduce_start(0, (gg, hh, gt))
 
-    def body(p, c):
+    def next_residual(p, c):
         resid[p] = resid[p] - START_STEP * grad[p]
         return c
 
-    planes(body, 0)
-    made = spill_send(3, resid)
+    planes(next_residual, 0)
+    made = spill_send(3, edge_rows(read_field(resid)), pack_columns(lambda p: resid[p]))
     waiting += made
-    variation(u_ext, ux, own_edge[0], keep_tv)
+    spread_and_slope(resid)
+    gradient_inside()
+    edge = packed_main(g_ext)
+    spill_fix(3, made)
+    made = send_gradient(4, edge)
+    waiting += made
     reduce_middle(0)
-    spill_wait(3, made)
-    gradient(g_ext)
-    halo_stage(4, g_ext, own_edge.at[1])
-    made = send(4)
-    waiting += made
-
-    def keep_spread(p, c):
-        resid[p] = spread[p, main, :]
-        return c
-
-    planes(keep_spread, 0)
-    halo_wait(4, made, g_ext, gx_halo)
-    blur_gradient()
+
+    def keep_pulled(p, extra):
+        add_main(p, extra)
+        resid[p] = spread[p] + extra
+
+    with_fix(keep_pulled)
+    clear_border(g_ext)
+    blur_inside(g_ext, keep_grad)
+    halo_fix(4, made, g_ext, gx_halo)
+    with_fix(add_grad)
     gg, hh, gt = sums_of_gradient()
     g2, h2, t2 = reduce_end(0)
     change_sq = START_STEP * START_STEP * g2
@@ -512,18 +574,17 @@
     gt = variation_dot(u_ext, ux, g_ext, gx_halo) - gt
     reduce_start(1, (gg, hh, gt))
 
-    made = spill_send(5, grad)
+    made = spill_send(5, edge_rows(read_field(grad)), pack_columns(lambda p: grad[p]))
     waiting += made
-    variation(u_ext, ux, own_edge[0], keep_tv)
+    spread_and_slope(grad)
+    spill_fix(5, made)
     reduce_middle(1)
-    spill_wait(5, made)
-
-    def last(p, c):
-        pulled = resid[p] - step * spread[p, main, :]
+
+    def last(p, extra):
+        pulled = resid[p] - step * (spread[p] + extra)
         g_ext[p, main, :] = pulled + WEIGHT_TV * tv[p] + DAMPING * u_ext[p, main, :]
-        return c
-
-    planes(last, 0)
+
+    with_fix(last)
     g2, h2, t2 = reduce_end(1)
     change_sq = step * step * g2
     change_growth = step * step * (h2 + DAMPING * g2) - step * WEIGHT_TV * t2
@@ -547,14 +608,14 @@
 def per_device(ny, nx, observed, profiles, tile_index):
     field = pltpu.VMEM((Z, CY, CX), F32)
     extended = pltpu.VMEM((Z, EXT, CX), F32)
+    matrix = pltpu.VMEM((2 * CX, 2 * CX), BF16)
     rounds = 6
     scratch = [
         extended, extended, field, field, field,
-        pltpu.VMEM((Z, CY + 32, CX), F32), extended, field,
-        pltpu.VMEM((Z * CY, 2 * CX), F32), pltpu.VMEM((40, CX), F32),
-        pltpu.VMEM((2 * CX, 2 * CX), BF16), pltpu.VMEM((2 * CX, 2 * CX), BF16),
-        pltpu.VMEM((CX, 2 * CX), BF16),
-        pltpu.VMEM((Z * CY, 2 * CX), BF16), pltpu.VMEM((Z * CY, 2 * CX), BF16),
+        pltpu.VMEM((Z, CY + 32, CX), F32), field,
+        pltpu.VMEM((Z * CY, CX), F32), pltpu.VMEM((40, CX), F32),
+        matrix, matrix, matrix, matrix,
+        pltpu.VMEM((Z, 16, CX), F32), pltpu.VMEM((Z * 8, CX), F32), pltpu.VMEM((CY, CX), F32),
         pltpu.VMEM((EXT, CX), F32), pltpu.VMEM((EXT, CX), F32),
         pltpu.VMEM((2, CY, CX), F32), pltpu.VMEM((CY + 32, CX), F32),
         pltpu.VMEM((rounds, 2, 8, 8, CX), F32), pltpu.VMEM((rounds, 2, 8, 8, CX), F32),

time: 63 us -> 60.2 us (0.956)
  Pallas kernels: 61.1 us -> 58.2 us
    pallas_call x1, Pallas kernels: 61.1 us -> 58.2 us  [per_device(): pl.pallas_call(functools.partial(kernel, ny, nx), out_shape=jax.ShapeDtyp...]
where the time goes in v3:
time: 60.2 us; the launch traced here: 59.9 us
  Pallas kernels  58.2 us (97%)
  local copies, waits for them, and re-layouts  1.67 us (3%)
    pallas_call x1, Pallas kernels, per_device(): pl.pallas_call(functools.partial(kernel, ny, nx), out_shape=jax.ShapeDtyp...  58.2 us
    unnamed x1, local copies, waits for them, and re-layouts  1.67 us

profile of v3, /device:TPU:1, one launch (start us, length us, event | category | flops | bytes accessed | tf_op | source)
XLA Modules:
  0.0 59.9 jit_solution(12920923376777209197)
XLA Ops:
  0.0 58.2 %shard_map.37 = f32[16,32,128]{2,1,0:T(8,128)} custom-call(f32[16,32,128]{2,1,0:T(8,128)} %obs_hbm.1, f32[9,3,64]{2,1,0:T(4,128)} %bitcast.1, s32[16,32]{1,0:T(8,128)} %tiles.1), custom_call_target="tpu_custom_call" | custom-call | tf_op jit(solution)/shard_map/pallas_call | solution.py:630
  58.2 1.7 %copy.5 = f32[16,32,128]{2,1,0:T(8,128)} copy(f32[16,32,128]{2,1,0:T(8,128)} %shard_map.37) | data formatting | bytes 524288

commit v4 on v3

--- a/solution.py
+++ b/solution.py
@@ -26,6 +26,7 @@
     obs_hbm, prof, tiles, out_ref,
     u_ext, g_ext, grad, tv, resid, back, spread, blur_y, flux,
     fwd, bwd, side_fwd, side_bwd, twice, y_fix, x_fix,
+    across_u, square, product, growth,
     ux, gx_halo, own_edge, edge_pad,
     send_y, recv_y, send_x, recv_x,
     part, all_x, part_y, all_y,
@@ -144,11 +145,24 @@
             )
         return made
 
-    def send(r):
+    def send_columns(r):
         made = copies(r)
-        for k in (4, 5, 6, 7, 2, 3, 0, 1):
+        for k in (4, 5, 6, 7, 2, 3):
             made[k].start()
         return made
+
+    def send_rows(made):
+        for k in (0, 1):
+            made[k].start()
+        return made
+
+    def wait_rows(made):
+        made[0].wait_recv()
+        made[1].wait_recv()
+
+    def wait_columns(made):
+        for k in (2, 3, 4, 5, 6, 7):
+            made[k].wait_recv()
 
     border = (lane < 4) | (lane >= CX - 4)
 
@@ -190,58 +204,68 @@
         return [jnp.where(low_half, read(p, 0), read(p, CY - 8)) for p in range(Z)]
 
     def halo_send(r, rows, edge):
-        put_rows(rows, send_y.at[r, 0], send_y.at[r, 1])
         send_x[r, pl.ds(8, CY), :] = edge
         send_x[r, pl.ds(0, 8), :] = edge[0:8]
         send_x[r, pl.ds(8 + CY, 8), :] = edge[CY - 8 : CY]
-        return send(r)
+        made = send_columns(r)
+        put_rows(rows(), send_y.at[r, 0], send_y.at[r, 1])
+        return send_rows(made)
 
     def halo_fix(r, made, ext, halo):
-        for c in made:
-            c.wait_recv()
+        wait_rows(made)
         rows = get_rows(recv_y.at[r, 1], recv_y.at[r, 0], last_row, first_row)
         for p in range(Z):
             ext[p, pl.ds(0, 8), :] = rows[p]
             ext[p, pl.ds(8 + CY, 8), :] = rows[p]
+        y_fix[...] = cross(rows, along, False, fwd)
+        wait_columns(made)
         halo[...] = sides(r, place < 4)
         edge = along[0] * halo[pl.ds(8 + RADIUS, CY), :]
         for b in range(1, TAPS):
             edge = edge + along[b] * halo[pl.ds(8 + RADIUS - b, CY), :]
         x_fix[...] = times(edge, side_fwd)
-        y_fix[...] = cross(rows, along, False, fwd)
 
     def spill_send(r, rows, edge):
         edge_pad[pl.ds(16, CY), :] = times(edge, side_bwd)
-        spilled = cross(rows, along[::-1], True, bwd)
-        put_rows([spilled[8 * p : 8 * p + 8] for p in range(Z)], send_y.at[r, 1], send_y.at[r, 0])
         total = along[0] * edge_pad[pl.ds(4, EXT), :]
         for b in range(1, TAPS):
             total = total + along[b] * edge_pad[pl.ds(4 + b, EXT), :]
         send_x[r] = total
-        return send(r)
+        made = send_columns(r)
+        spilled = cross(rows(), along[::-1], True, bwd)
+        put_rows([spilled[8 * p : 8 * p + 8] for p in range(Z)], send_y.at[r, 1], send_y.at[r, 0])
+        return send_rows(made)
 
     def spill_fix(r, made):
-        for c in made:
-            c.wait_recv()
+        wait_rows(made)
         rows = get_rows(recv_y.at[r, 0], recv_y.at[r, 1], first_row, last_row)
         y_fix[...] = jnp.concatenate(rows, axis=0)
+        wait_columns(made)
         both = sides(r, place >= 4)
         x_fix[pl.ds(0, 8), :] = both[8:16] + both[0:8]
         x_fix[pl.ds(8, 16), :] = both[16:CY]
         x_fix[pl.ds(24, 8), :] = both[CY : CY + 8] + both[CY + 8 : CY + 16]
 
-    def fixed_edges(read, edge):
-        extra = x_fix[...]
-        ends = jnp.where(low_half, extra[0:8], extra[CY - 8 : CY])
-        rows, packed = edge_rows(read), jnp.zeros((8, CX), F32)
-        for p in range(Z):
-            y = y_fix[pl.ds(8 * p, 8), :]
-            packed = jnp.where(plane_of == p, pltpu.roll(y, 8 * p + 4, 1), packed)
-            rows[p] = rows[p] + y + jnp.where(border, pltpu.roll(ends, 124 - 8 * p, 1), 0.0)
-        edge = edge + extra
+    def packed_rows_fix():
+        packed = jnp.zeros((8, CX), F32)
+        for p in range(Z):
+            packed = jnp.where(plane_of == p, pltpu.roll(y_fix[pl.ds(8 * p, 8), :], 8 * p + 4, 1), packed)
+        return packed
+
+    def fixed_columns(edge):
+        packed = packed_rows_fix()
+        edge = edge + x_fix[...]
         top = edge[0:8] + jnp.where(low_half, packed, 0.0)
         low = edge[CY - 8 : CY] + jnp.where(low_half, 0.0, packed)
-        return rows, jnp.concatenate([top, edge[8 : CY - 8], low], axis=0)
+        return jnp.concatenate([top, edge[8 : CY - 8], low], axis=0)
+
+    def fixed_rows(read):
+        ends = jnp.where(low_half, x_fix[pl.ds(0, 8), :], x_fix[pl.ds(CY - 8, 8), :])
+        rows = edge_rows(read)
+        for p in range(Z):
+            extra = jnp.where(border, pltpu.roll(ends, 124 - 8 * p, 1), 0.0)
+            rows[p] = rows[p] + y_fix[pl.ds(8 * p, 8), :] + extra
+        return rows
 
     def with_fix(add):
         extra = x_fix[...]
@@ -304,6 +328,8 @@
                 total = total + along[b] * back[p, pl.ds(12 + b, CY), :]
             write(p, total)
 
+    zero8 = jnp.zeros((8, CX), F32)
+    main = pl.ds(8, CY)
     rows40 = lax.broadcasted_iota(jnp.int32, (40, CX), 0)
     rows32 = lax.broadcasted_iota(jnp.int32, (CY, CX), 0)
     no_row_diff = last_row & (rows40 == 39)
@@ -346,26 +372,52 @@
     def rows8(value):
         return value[0:8] + value[8:16] + value[16:24] + value[24:32]
 
-    def variation_dot(ext, halo, other, other_halo):
-        around, other_around = halo[pl.ds(8, CY), :], other_halo[pl.ds(8, CY), :]
-        final_row = last_row & (rows32 == CY - 1)
-
-        def shifted(u, side, p):
-            beyond = pltpu.roll(side, 124 - 8 * p, 1)
-            return pltpu.roll(jnp.where(lane == 0, beyond, u), CX - 1, 1) - u
+    final_lane = lane == CX - 1
+    next_lane = final_lane & jnp.logical_not(last_col)
+    next_row = (sub8 == 7) & jnp.logical_not(last_row)
+
+    def tension_inside():
+        around = ux[pl.ds(8, CY), :]
 
         def body(p, total):
-            u, g = ext[p, pl.ds(8, CY), :], other[p, pl.ds(8, CY), :]
+            u, g = u_ext[p, main, :], g_ext[p, main, :]
             after = min(p + 1, Z - 1) if isinstance(p, int) else jnp.minimum(p + 1, Z - 1)
-            dz = ext[after, pl.ds(8, CY), :] - u
-            ez = other[after, pl.ds(8, CY), :] - g
-            dy = jnp.where(final_row, 0.0, ext[p, pl.ds(9, CY), :] - u)
-            ey = other[p, pl.ds(9, CY), :] - g
-            dx = jnp.where(no_col_diff, 0.0, shifted(u, around, p))
-            ex = shifted(g, other_around, p)
-            return total + rows8((dx * ex + dy * ey + dz * ez) * inverse_size(dx, dy, dz))
-
-        return planes(body, jnp.zeros((8, CX), F32), 4)
+            dz = u_ext[after, main, :] - u
+            ez = g_ext[after, main, :] - g
+            dy = jnp.where(last_row & (rows32 == CY - 1), 0.0, u_ext[p, pl.ds(9, CY), :] - u)
+            ey = jnp.where(rows32 == CY - 1, 0.0, g_ext[p, pl.ds(9, CY), :] - g)
+            beyond = pltpu.roll(around, 124 - 8 * p, 1)
+            dx = pltpu.roll(jnp.where(lane == 0, beyond, u), CX - 1, 1) - u
+            dx = jnp.where(no_col_diff, 0.0, dx)
+            ex = jnp.where(final_lane, 0.0, pltpu.roll(g, CX - 1, 1) - g)
+            across_u[p] = dx
+            square[p] = dx * dx + dy * dy + dz * dz + SMOOTHING * SMOOTHING
+            product[p] = dx * ex + dy * ey + dz * ez
+            growth[p] = ex * ex + ey * ey + ez * ez
+            return total[0] + rows8(g * g), total[1] + rows8(g * tv[p])
+
+        return planes(body, (zero8, zero8))
+
+    def tension_border():
+        around = gx_halo[pl.ds(8, CY), :]
+        for p in range(Z):
+            ex = jnp.where(next_lane, pltpu.roll(around, 123 - 8 * p, 1) - g_ext[p, main, :], 0.0)
+            product[p] = product[p] + across_u[p] * ex
+            growth[p] = growth[p] + ex * ex
+            bottom = pl.ds(CY - 8, 8)
+            ey = jnp.where(next_row, g_ext[p, pl.ds(CY + 1, 8), :] - g_ext[p, pl.ds(CY, 8), :], 0.0)
+            dy = u_ext[p, pl.ds(CY + 1, 8), :] - u_ext[p, pl.ds(CY, 8), :]
+            product[p, bottom, :] = product[p, bottom, :] + dy * ey
+            growth[p, bottom, :] = growth[p, bottom, :] + ey * ey
+
+    def tension_sum(step):
+        total = zero8
+        for p in range(Z):
+            part_ = product[p] - step * growth[p]
+            size = square[p] - step * (product[p] + part_)
+            size = jnp.maximum(size, SMOOTHING * SMOOTHING)
+            total = total + rows8(part_ * lax.rsqrt(size))
+        return total
 
     def fold(values):
         total = jnp.zeros((1, CX), F32)
@@ -420,9 +472,6 @@
         total = jnp.sum(all_y[a], axis=0)
         return [jnp.sum(jnp.where(lane // 32 == i, total, 0.0), axis=1, keepdims=True) for i in range(3)]
 
-    zero8 = jnp.zeros((8, CX), F32)
-    main = pl.ds(8, CY)
-
     def tell(level, distance):
         for axis, n in enumerate((ny, nx)):
             if n // 2 > distance:
@@ -461,8 +510,18 @@
     def add_main(p, extra):
         g_ext[p, main, :] = g_ext[p, main, :] + extra
 
-    def add_grad(p, extra):
-        grad[p] = grad[p] + extra
+    def finish_blur():
+        sums = []
+
+        def add(p, extra):
+            h = grad[p] + extra
+            grad[p] = h
+            sums.append(rows8(h * h))
+
+        with_fix(add)
+        while len(sums) > 1:
+            sums = [x + y for x, y in zip(sums[::2], sums[1::2])]
+        return sums[0]
 
     def add_resid(p, extra):
         resid[p] = resid[p] + extra
@@ -481,29 +540,20 @@
         planes(body, 0)
 
     def send_gradient(r, edge):
-        rows, edge = fixed_edges(read_main(g_ext), edge)
+        edge = fixed_columns(edge)
         own_edge[1] = edge
-        return halo_send(r, rows, edge)
+        return halo_send(r, lambda: fixed_rows(read_main(g_ext)), edge)
 
     def spread_and_slope(field):
         spread_inside(field, keep_spread)
         variation(u_ext, ux, own_edge[0], keep_tv)
-
-    def sums_of_gradient():
-        def body(p, c):
-            g = g_ext[p, main, :]
-            h = grad[p]
-            return c[0] + rows8(g * g), c[1] + rows8(h * h), c[2] + rows8(g * tv[p])
-
-        return planes(body, (zero8, zero8, zero8))
 
     waiting = []
     clear_border(u_ext)
     edge = packed_main(u_ext)
     own_edge[0] = edge
-    rows = edge_rows(read_main(u_ext))
     pl.semaphore_wait(barrier, len(SIDES))
-    made = halo_send(0, rows, edge)
+    made = halo_send(0, lambda: edge_rows(read_main(u_ext)), edge)
     waiting += made
     prepare()
 
@@ -513,8 +563,7 @@
     blur_inside(u_ext, keep_residual)
     edge = pack_columns(lambda p: resid[p])
     halo_fix(0, made, u_ext, ux)
-    rows, edge = fixed_edges(read_field(resid), edge)
-    made = spill_send(1, rows, edge)
+    made = spill_send(1, lambda: fixed_rows(read_field(resid)), fixed_columns(edge))
     waiting += made
     tell(0, 2)
     with_fix(add_resid)
@@ -529,14 +578,13 @@
     with_fix(add_main)
     clear_border(g_ext)
     blur_inside(g_ext, keep_grad)
+    gg, gt = tension_inside()
     halo_fix(2, made, g_ext, gx_halo)
     hear(1, 4)
     tell(2, 8)
-    with_fix(add_grad)
-
-    advance(START_STEP)
-    gg, hh, gt = sums_of_gradient()
-    gt = variation_dot(u_ext, ux, g_ext, gx_halo) - gt
+    hh = finish_blur()
+    tension_border()
+    gt = tension_sum(START_STEP) - gt
     hear(2, 8)
     reduce_start(0, (gg, hh, gt))
 
@@ -545,8 +593,9 @@
         return c
 
     planes(next_residual, 0)
-    made = spill_send(3, edge_rows(read_field(resid)), pack_columns(lambda p: resid[p]))
+    made = spill_send(3, lambda: edge_rows(read_field(resid)), pack_columns(lambda p: resid[p]))
     waiting += made
+    advance(START_STEP)
     spread_and_slope(resid)
     gradient_inside()
     edge = packed_main(g_ext)
@@ -562,20 +611,21 @@
     with_fix(keep_pulled)
     clear_border(g_ext)
     blur_inside(g_ext, keep_grad)
+    gg, gt = tension_inside()
     halo_fix(4, made, g_ext, gx_halo)
-    with_fix(add_grad)
-    gg, hh, gt = sums_of_gradient()
+    hh = finish_blur()
+    tension_border()
     g2, h2, t2 = reduce_end(0)
     change_sq = START_STEP * START_STEP * g2
     change_growth = START_STEP * START_STEP * (h2 + DAMPING * g2) - START_STEP * WEIGHT_TV * t2
     step = change_sq / change_growth
 
+    gt = tension_sum(step) - gt
+    reduce_start(1, (gg, hh, gt))
+
+    made = spill_send(5, lambda: edge_rows(read_field(grad)), pack_columns(lambda p: grad[p]))
+    waiting += made
     advance(step)
-    gt = variation_dot(u_ext, ux, g_ext, gx_halo) - gt
-    reduce_start(1, (gg, hh, gt))
-
-    made = spill_send(5, edge_rows(read_field(grad)), pack_columns(lambda p: grad[p]))
-    waiting += made
     spread_and_slope(grad)
     spill_fix(5, made)
     reduce_middle(1)
@@ -616,6 +666,7 @@
         pltpu.VMEM((Z * CY, CX), F32), pltpu.VMEM((40, CX), F32),
         matrix, matrix, matrix, matrix,
         pltpu.VMEM((Z, 16, CX), F32), pltpu.VMEM((Z * 8, CX), F32), pltpu.VMEM((CY, CX), F32),
+        field, field, field, field,
         pltpu.VMEM((EXT, CX), F32), pltpu.VMEM((EXT, CX), F32),
         pltpu.VMEM((2, CY, CX), F32), pltpu.VMEM((CY + 32, CX), F32),
         pltpu.VMEM((rounds, 2, 8, 8, CX), F32), pltpu.VMEM((rounds, 2, 8, 8, CX), F32),

time: 60.2 us -> 58.6 us (0.973)
  Pallas kernels: 58.2 us -> 56.4 us
    pallas_call x1, Pallas kernels: 58.2 us -> 56.4 us  [per_device(): pl.pallas_call(functools.partial(kernel, ny, nx), out_shape=jax.ShapeDtyp...]
where the time goes in v4:
time: 58.6 us; the launch traced here: 58.1 us
  Pallas kernels  56.4 us (96%)
  local copies, waits for them, and re-layouts  1.67 us (3%)
    pallas_call x1, Pallas kernels, per_device(): pl.pallas_call(functools.partial(kernel, ny, nx), out_shape=jax.ShapeDtyp...  56.4 us
    unnamed x1, local copies, waits for them, and re-layouts  1.67 us

profile of v4, /device:TPU:1, one launch (start us, length us, event | category | flops | bytes accessed | tf_op | source)
XLA Modules:
  0.0 58.1 jit_solution(17612682136135027120)
XLA Ops:
  0.0 56.4 %shard_map.37 = f32[16,32,128]{2,1,0:T(8,128)} custom-call(f32[16,32,128]{2,1,0:T(8,128)} %obs_hbm.1, f32[9,3,64]{2,1,0:T(4,128)} %bitcast.1, s32[16,32]{1,0:T(8,128)} %tiles.1), custom_call_target="tpu_custom_call" | custom-call | tf_op jit(solution)/shard_map/pallas_call | solution.py:681
  56.5 1.7 %copy.5 = f32[16,32,128]{2,1,0:T(8,128)} copy(f32[16,32,128]{2,1,0:T(8,128)} %shard_map.37) | data formatting | bytes 524288

commit v5 on v4

--- a/solution.py
+++ b/solution.py
@@ -23,14 +23,15 @@
 
 def kernel(
     ny, nx,
-    obs_hbm, prof, tiles, out_ref,
+    obs_hbm, prof_hbm, tiles_hbm, u_out, g_out, step_out,
+    prof, tiles,
     u_ext, g_ext, grad, tv, resid, back, spread, blur_y, flux,
     fwd, bwd, side_fwd, side_bwd, twice, y_fix, x_fix,
     across_u, square, product, growth,
     ux, gx_halo, own_edge, edge_pad,
     send_y, recv_y, send_x, recv_x,
     part, all_x, part_y, all_y,
-    load_sem, send_sem, recv_sem, ar_send, ar_recv, known,
+    load_sem, table_sem, store_sem, send_sem, recv_sem, ar_send, ar_recv, known,
 ):
     row = lax.axis_index("gy")
     col = lax.axis_index("gx")
@@ -43,16 +44,17 @@
 
     load = pltpu.make_async_copy(obs_hbm, u_ext.at[:, pl.ds(8, CY), :], load_sem)
     load.start()
+    table_loads = (
+        pltpu.make_async_copy(prof_hbm, prof, table_sem.at[0]),
+        pltpu.make_async_copy(tiles_hbm, tiles, table_sem.at[1]),
+    )
+    table_loads[0].start()
+    table_loads[1].start()
 
     barrier = pltpu.get_barrier_semaphore()
 
     for dy, dx in SIDES:
         pl.semaphore_signal(barrier, inc=1, device_id=at(dy, dx), device_id_type=MESH)
-
-    number = tiles[row, col]
-    depth = [prof[a, 0, number] for a in range(TAPS)]
-    along = [prof[a, 1, number] for a in range(TAPS)]
-    across = [prof[a, 2, number] for a in range(TAPS)]
 
     lane = lax.broadcasted_iota(jnp.int32, (1, CX), 1)
     sub8 = lax.broadcasted_iota(jnp.int32, (8, CX), 0)
@@ -211,14 +213,22 @@
         put_rows(rows(), send_y.at[r, 0], send_y.at[r, 1])
         return send_rows(made)
 
-    def halo_fix(r, made, ext, halo):
+    def halo_fix(r, made, ext, halo, between=None):
         wait_rows(made)
         rows = get_rows(recv_y.at[r, 1], recv_y.at[r, 0], last_row, first_row)
         for p in range(Z):
             ext[p, pl.ds(0, 8), :] = rows[p]
             ext[p, pl.ds(8 + CY, 8), :] = rows[p]
         y_fix[...] = cross(rows, along, False, fwd)
-        wait_columns(made)
+        if between is not None:
+            made[2].wait_recv()
+            made[3].wait_recv()
+            halo[pl.ds(8, CY), :] = sides(r, place < 4, 8, CY)
+            between()
+            for k in (4, 5, 6, 7):
+                made[k].wait_recv()
+        else:
+            wait_columns(made)
         halo[...] = sides(r, place < 4)
         edge = along[0] * halo[pl.ds(8 + RADIUS, CY), :]
         for b in range(1, TAPS):
@@ -276,10 +286,12 @@
             low = e[CY - 8 : CY] + jnp.where(low_half, 0.0, y)
             add(p, jnp.concatenate([top, e[8 : CY - 8], low], axis=0))
 
-    def sides(r, from_left):
-        left = jnp.where(first_col, 0.0, recv_x[r, 0])
-        right = jnp.where(last_col, 0.0, recv_x[r, 1])
+    def sides(r, from_left, start=0, size=EXT):
+        left = jnp.where(first_col, 0.0, recv_x[r, 0, pl.ds(start, size), :])
+        right = jnp.where(last_col, 0.0, recv_x[r, 1, pl.ds(start, size), :])
         both = jnp.where(from_left, left, right)
+        if size < EXT:
+            return both
         at_row = lax.broadcasted_iota(jnp.int32, (EXT, CX), 0)
         both = jnp.where(first_row & (at_row < 8), 0.0, both)
         return jnp.where(last_row & (at_row >= 8 + CY), 0.0, both)
@@ -555,6 +567,12 @@
     pl.semaphore_wait(barrier, len(SIDES))
     made = halo_send(0, lambda: edge_rows(read_main(u_ext)), edge)
     waiting += made
+    table_loads[0].wait()
+    table_loads[1].wait()
+    number = tiles[row, col]
+    depth = [prof[a, 0, number] for a in range(TAPS)]
+    along = [prof[a, 1, number] for a in range(TAPS)]
+    across = [prof[a, 2, number] for a in range(TAPS)]
     prepare()
 
     def keep_residual(p, t, value):
@@ -579,12 +597,17 @@
     clear_border(g_ext)
     blur_inside(g_ext, keep_grad)
     gg, gt = tension_inside()
-    halo_fix(2, made, g_ext, gx_halo)
+    sums = []
+
+    def tension():
+        tension_border()
+        sums.append(tension_sum(START_STEP))
+
+    halo_fix(2, made, g_ext, gx_halo, tension)
     hear(1, 4)
     tell(2, 8)
     hh = finish_blur()
-    tension_border()
-    gt = tension_sum(START_STEP) - gt
+    gt = sums[0] - gt
     hear(2, 8)
     reduce_start(0, (gg, hh, gt))
 
@@ -612,9 +635,8 @@
     clear_border(g_ext)
     blur_inside(g_ext, keep_grad)
     gg, gt = tension_inside()
-    halo_fix(4, made, g_ext, gx_halo)
+    halo_fix(4, made, g_ext, gx_halo, tension_border)
     hh = finish_blur()
-    tension_border()
     g2, h2, t2 = reduce_end(0)
     change_sq = START_STEP * START_STEP * g2
     change_growth = START_STEP * START_STEP * (h2 + DAMPING * g2) - START_STEP * WEIGHT_TV * t2
@@ -626,6 +648,8 @@
     made = spill_send(5, lambda: edge_rows(read_field(grad)), pack_columns(lambda p: grad[p]))
     waiting += made
     advance(step)
+    u_store = pltpu.make_async_copy(u_ext.at[:, main, :], u_out, store_sem.at[0])
+    u_store.start()
     spread_and_slope(grad)
     spill_fix(5, made)
     reduce_middle(1)
@@ -635,17 +659,8 @@
         g_ext[p, main, :] = pulled + WEIGHT_TV * tv[p] + DAMPING * u_ext[p, main, :]
 
     with_fix(last)
-    g2, h2, t2 = reduce_end(1)
-    change_sq = step * step * g2
-    change_growth = step * step * (h2 + DAMPING * g2) - step * WEIGHT_TV * t2
-    step = change_sq / change_growth
-
-    def finish(p, c):
-        out_ref[p] = u_ext[p, main, :] - step * g_ext[p, main, :]
-        return c
-
-    planes(finish, 0)
-
+    g_store = pltpu.make_async_copy(g_ext.at[:, main, :], g_out, store_sem.at[1])
+    g_store.start()
     for c in waiting:
         c.wait_send()
     for a in range(2):
@@ -653,6 +668,12 @@
         pltpu.make_async_copy(got, got, ar_send.at[a, 0]).wait()
         got = all_y.at[a, pl.ds(0, ny - 1)]
         pltpu.make_async_copy(got, got, ar_send.at[a, 1]).wait()
+    u_store.wait()
+    g_store.wait()
+    g2, h2, t2 = reduce_end(1)
+    change_sq = step * step * g2
+    change_growth = step * step * (h2 + DAMPING * g2) - step * WEIGHT_TV * t2
+    step_out[...] = jnp.broadcast_to(change_sq / change_growth, (1, CX))
 
 
 def per_device(ny, nx, observed, profiles, tile_index):
@@ -661,6 +682,7 @@
     matrix = pltpu.VMEM((2 * CX, 2 * CX), BF16)
     rounds = 6
     scratch = [
+        pltpu.SMEM((TAPS, 3, profiles.shape[0]), F32), pltpu.SMEM((ny, nx), jnp.int32),
         extended, extended, field, field, field,
         pltpu.VMEM((Z, CY + 32, CX), F32), field,
         pltpu.VMEM((Z * CY, CX), F32), pltpu.VMEM((40, CX), F32),
@@ -673,23 +695,29 @@
         pltpu.VMEM((rounds, EXT, CX), F32), pltpu.VMEM((rounds, 2, EXT, CX), F32),
         pltpu.VMEM((2, 1, CX), F32), pltpu.VMEM((2, nx, 1, CX), F32),
         pltpu.VMEM((2, 1, CX), F32), pltpu.VMEM((2, ny, 1, CX), F32),
-        pltpu.SemaphoreType.DMA,
+        pltpu.SemaphoreType.DMA, pltpu.SemaphoreType.DMA((2,)), pltpu.SemaphoreType.DMA((2,)),
         pltpu.SemaphoreType.DMA((rounds, 8)), pltpu.SemaphoreType.DMA((rounds, 8)),
         pltpu.SemaphoreType.DMA((2, 2)), pltpu.SemaphoreType.DMA((2, 2)),
         pltpu.SemaphoreType.REGULAR((2, 3)),
     ]
-    return pl.pallas_call(
+    whole = jax.ShapeDtypeStruct((Z, CY, CX), F32)
+    estimate, gradient, step = pl.pallas_call(
         functools.partial(kernel, ny, nx),
-        out_shape=jax.ShapeDtypeStruct((Z, CY, CX), F32),
+        out_shape=(whole, whole, jax.ShapeDtypeStruct((1, CX), F32)),
         in_specs=[
             pl.BlockSpec(memory_space=pl.ANY),
-            pl.BlockSpec(memory_space=pltpu.SMEM),
-            pl.BlockSpec(memory_space=pltpu.SMEM),
+            pl.BlockSpec(memory_space=pl.ANY),
+            pl.BlockSpec(memory_space=pl.ANY),
         ],
-        out_specs=pl.BlockSpec(memory_space=pltpu.VMEM),
+        out_specs=(
+            pl.BlockSpec(memory_space=pl.ANY),
+            pl.BlockSpec(memory_space=pl.ANY),
+            pl.BlockSpec(memory_space=pltpu.VMEM),
+        ),
         scratch_shapes=scratch,
         compiler_params=pltpu.CompilerParams(collective_id=0, has_side_effects=True),
     )(observed, jnp.transpose(profiles, (2, 1, 0)), tile_index)
+    return estimate - step[0] * gradient
 
 
 def solution(mesh):

time: 58.6 us -> 58 us (0.990)
  other arithmetic: 0 us -> 1.77 us
  Pallas kernels: 56.4 us -> 55.3 us
  local copies, waits for them, and re-layouts: 1.67 us -> 0.66 us
    sub x0 -> x1, other arithmetic: none -> 1.77 us  [per_device(): return estimate - step[0] * gradient]
    pallas_call x1, Pallas kernels: 56.4 us -> 55.3 us  [per_device(): pl.pallas_call(functools.partial(kernel, ny, nx), out_shape=(whole, whole...]
    unnamed x1 -> x2, local copies, waits for them, and re-layouts: 1.67 us -> 0.66 us
where the time goes in v5:
time: 58 us; the launch traced here: 57.7 us
  Pallas kernels  55.3 us (95%)
  other arithmetic  1.77 us (3%)
  local copies, waits for them, and re-layouts  0.66 us (1%)
    pallas_call x1, Pallas kernels, per_device(): pl.pallas_call(functools.partial(kernel, ny, nx), out_shape=(whole, whole...  55.3 us
    sub x1, other arithmetic, per_device(): return estimate - step[0] * gradient  1.77 us

profile of v5, /device:TPU:1, one launch (start us, length us, event | category | flops | bytes accessed | tf_op | source)
XLA Modules:
  0.0 57.7 jit_solution(4374021077353264790)
XLA Ops:
  0.0 55.3 %shard_map.37 = (f32[16,32,128]{2,1,0:T(8,128)}, f32[16,32,128]{2,1,0:T(8,128)}, f32[1,128]{1,0:T(1,128)}) custom-call(f32[16,32,128]{2,1,0:T(8,128)} %obs_hbm.1, f32[9,3,64]{2,1,0:T(4,128)} %bitcast.2, s32[16,32]{1,0:T(8,128)} %tiles_hbm.1), custom_call_target="tpu_custom_call" | custom-call | tf_op jit(solution)/shard_map/pallas_call | solution.py:704
  55.3 0.0 copy-start
  55.3 0.7 %copy-done = f32[1,128]{1,0:T(1,128)S(1)} copy-done((f32[1,128]{1,0:T(1,128)S(1)}, f32[1,128]{1,0:T(1,128)}, u32[]{:S(2)}) %copy-start) | copy-done | bytes 536
  56.0 1.8 %multiply_subtract_fusion = f32[16,32,128]{2,1,0:T(8,128)} fusion(f32[16,32,128]{2,1,0:T(8,128)} %get-tuple-element.8, f32[16,32,128]{2,1,0:T(8,128)} %get-tuple-element.10, f32[128]{0:T(128)S(1)} %bitcast.3), kind=kLoop, calls=%fused_computation | loop fusion | flops 131072 | bytes 786944 | tf_op jit(solution)/shard_map/sub | solution.py:720
Async XLA Ops:
  55.3 0.7 %copy-start = (f32[1,128]{1,0:T(1,128)S(1)}, f32[1,128]{1,0:T(1,128)}, u32[]{:S(2)}) copy-start(f32[1,128]{1,0:T(1,128)} %get-tuple-element.9) | copy-start | bytes 1540

commit v6 on v5

--- a/solution.py
+++ b/solution.py
@@ -31,7 +31,7 @@
     ux, gx_halo, own_edge, edge_pad,
     send_y, recv_y, send_x, recv_x,
     part, all_x, part_y, all_y,
-    load_sem, table_sem, store_sem, send_sem, recv_sem, ar_send, ar_recv, known,
+    load_sem, table_sem, send_sem, recv_sem, ar_send, ar_recv, known,
 ):
     row = lax.axis_index("gy")
     col = lax.axis_index("gx")
@@ -648,19 +648,17 @@
     made = spill_send(5, lambda: edge_rows(read_field(grad)), pack_columns(lambda p: grad[p]))
     waiting += made
     advance(step)
-    u_store = pltpu.make_async_copy(u_ext.at[:, main, :], u_out, store_sem.at[0])
-    u_store.start()
     spread_and_slope(grad)
     spill_fix(5, made)
     reduce_middle(1)
 
     def last(p, extra):
         pulled = resid[p] - step * (spread[p] + extra)
-        g_ext[p, main, :] = pulled + WEIGHT_TV * tv[p] + DAMPING * u_ext[p, main, :]
+        u = u_ext[p, main, :]
+        u_out[p] = u
+        g_out[p] = pulled + WEIGHT_TV * tv[p] + DAMPING * u
 
     with_fix(last)
-    g_store = pltpu.make_async_copy(g_ext.at[:, main, :], g_out, store_sem.at[1])
-    g_store.start()
     for c in waiting:
         c.wait_send()
     for a in range(2):
@@ -668,8 +666,6 @@
         pltpu.make_async_copy(got, got, ar_send.at[a, 0]).wait()
         got = all_y.at[a, pl.ds(0, ny - 1)]
         pltpu.make_async_copy(got, got, ar_send.at[a, 1]).wait()
-    u_store.wait()
-    g_store.wait()
     g2, h2, t2 = reduce_end(1)
     change_sq = step * step * g2
     change_growth = step * step * (h2 + DAMPING * g2) - step * WEIGHT_TV * t2
@@ -695,29 +691,35 @@
         pltpu.VMEM((rounds, EXT, CX), F32), pltpu.VMEM((rounds, 2, EXT, CX), F32),
         pltpu.VMEM((2, 1, CX), F32), pltpu.VMEM((2, nx, 1, CX), F32),
         pltpu.VMEM((2, 1, CX), F32), pltpu.VMEM((2, ny, 1, CX), F32),
-        pltpu.SemaphoreType.DMA, pltpu.SemaphoreType.DMA((2,)), pltpu.SemaphoreType.DMA((2,)),
+        pltpu.SemaphoreType.DMA, pltpu.SemaphoreType.DMA((2,)),
         pltpu.SemaphoreType.DMA((rounds, 8)), pltpu.SemaphoreType.DMA((rounds, 8)),
         pltpu.SemaphoreType.DMA((2, 2)), pltpu.SemaphoreType.DMA((2, 2)),
         pltpu.SemaphoreType.REGULAR((2, 3)),
     ]
-    whole = jax.ShapeDtypeStruct((Z, CY, CX), F32)
+    whole = pltpu.VMEM((Z, CY, CX), F32)
     estimate, gradient, step = pl.pallas_call(
         functools.partial(kernel, ny, nx),
-        out_shape=(whole, whole, jax.ShapeDtypeStruct((1, CX), F32)),
-        in_specs=[
-            pl.BlockSpec(memory_space=pl.ANY),
-            pl.BlockSpec(memory_space=pl.ANY),
-            pl.BlockSpec(memory_space=pl.ANY),
-        ],
-        out_specs=(
-            pl.BlockSpec(memory_space=pl.ANY),
-            pl.BlockSpec(memory_space=pl.ANY),
-            pl.BlockSpec(memory_space=pltpu.VMEM),
+        out_shape=(whole, whole, pltpu.VMEM((1, CX), F32)),
+        in_specs=[pl.BlockSpec(memory_space=pltpu.HBM)] * 3,
+        out_specs=(pl.BlockSpec(memory_space=pltpu.VMEM),) * 3,
+        scratch_shapes=scratch,
+        compiler_params=pltpu.CompilerParams(
+            collective_id=0, has_side_effects=True
         ),
-        scratch_shapes=scratch,
-        compiler_params=pltpu.CompilerParams(collective_id=0, has_side_effects=True),
     )(observed, jnp.transpose(profiles, (2, 1, 0)), tile_index)
-    return estimate - step[0] * gradient
+    return pl.pallas_call(
+        last_update,
+        out_shape=jax.ShapeDtypeStruct((Z, CY, CX), F32),
+        in_specs=[pl.BlockSpec(memory_space=pltpu.VMEM)] * 3,
+        out_specs=pl.BlockSpec(memory_space=pltpu.VMEM),
+        compiler_params=pltpu.CompilerParams(vmem_limit_bytes=24 << 20),
+    )(estimate, gradient, step)
+
+
+def last_update(u, g, step, out_ref):
+    t = step[...]
+    for p in range(Z):
+        out_ref[p] = u[p] - t * g[p]
 
 
 def solution(mesh):

time: 58 us -> 55.6 us (0.959)
  other arithmetic: 1.77 us -> 0 us
  local copies, waits for them, and re-layouts: 0.66 us -> 0 us
    sub x1 -> x0, other arithmetic: 1.77 us -> none  [per_device(): return estimate - step[0] * gradient]
    pallas_call x0 -> x1, Pallas kernels: none -> 0.73 us  [per_device(): pl.pallas_call(last_update, out_shape=jax.ShapeDtypeStruct((Z, CY, CX), F...]
    unnamed x2 -> x0, local copies, waits for them, and re-layouts: 0.66 us -> none
    pallas_call x1, Pallas kernels: 55.3 us -> 54.7 us  [per_device(): pl.pallas_call(functools.partial(kernel, ny, nx), out_shape=(whole, whole...]
where the time goes in v6:
time: 55.6 us; the launch traced here: 55.4 us
  Pallas kernels  55.4 us (100%)
    pallas_call x1, Pallas kernels, per_device(): pl.pallas_call(functools.partial(kernel, ny, nx), out_shape=(whole, whole...  54.7 us

profile of v6, /device:TPU:1, one launch (start us, length us, event | category | flops | bytes accessed | tf_op | source)
XLA Modules:
  0.0 55.4 jit_solution(839285691784388160)
XLA Ops:
  0.0 54.7 %shard_map.37 = (f32[16,32,128]{2,1,0:T(8,128)S(1)}, f32[16,32,128]{2,1,0:T(8,128)S(1)}, f32[1,128]{1,0:T(1,128)S(1)}) custom-call(f32[16,32,128]{2,1,0:T(8,128)} %obs_hbm.1, f32[9,3,64]{2,1,0:T(4,128)} %bitcast.1, s32[16,32]{1,0:T(8,128)} %tiles_hbm.1), custom_call_target="tpu_custom_call" | custom-call | tf_op jit(solution)/shard_map/pallas_call | solution.py:700
  54.7 0.7 %shard_map.38 = f32[16,32,128]{2,1,0:T(8,128)} custom-call(f32[16,32,128]{2,1,0:T(8,128)S(1)} %get-tuple-element.8.u, f32[16,32,128]{2,1,0:T(8,128)S(1)} %get-tuple-element.9.g, f32[1,128]{1,0:T(1,128)S(1)} %get-tuple-element.10.step), custom_call_target="tpu_custom_call" | custom-call | tf_op jit(solution)/shard_map/pallas_call | solution.py:710

commit v7 on v6

--- a/solution.py
+++ b/solution.py
@@ -484,18 +484,18 @@
         total = jnp.sum(all_y[a], axis=0)
         return [jnp.sum(jnp.where(lane // 32 == i, total, 0.0), axis=1, keepdims=True) for i in range(3)]
 
-    def tell(level, distance):
+    def tell(level, distance, axes=(0, 1)):
         for axis, n in enumerate((ny, nx)):
-            if n // 2 > distance:
+            if axis in axes and n // 2 > distance:
                 for d in (-distance, distance):
                     pl.semaphore_signal(
                         known.at[axis, level], inc=1,
                         device_id=at(d, 0) if axis == 0 else at(0, d), device_id_type=MESH,
                     )
 
-    def hear(level, distance):
+    def hear(level, distance, axes=(0, 1)):
         for axis, n in enumerate((ny, nx)):
-            if n // 2 > distance:
+            if axis in axes and n // 2 > distance:
                 pl.semaphore_wait(known.at[axis, level], 2)
 
     def keep_tv(p, slope):
@@ -597,6 +597,8 @@
     clear_border(g_ext)
     blur_inside(g_ext, keep_grad)
     gg, gt = tension_inside()
+    hear(1, 4, (1,))
+    tell(2, 8)
     sums = []
 
     def tension():
@@ -604,8 +606,6 @@
         sums.append(tension_sum(START_STEP))
 
     halo_fix(2, made, g_ext, gx_halo, tension)
-    hear(1, 4)
-    tell(2, 8)
     hh = finish_blur()
     gt = sums[0] - gt
     hear(2, 8)
@@ -622,10 +622,11 @@
     spread_and_slope(resid)
     gradient_inside()
     edge = packed_main(g_ext)
+    hear(1, 4, (0,))
+    reduce_middle(0)
     spill_fix(3, made)
     made = send_gradient(4, edge)
     waiting += made
-    reduce_middle(0)
 
     def keep_pulled(p, extra):
         add_main(p, extra)
@@ -649,8 +650,8 @@
     waiting += made
     advance(step)
     spread_and_slope(grad)
+    reduce_middle(1)
     spill_fix(5, made)
-    reduce_middle(1)
 
     def last(p, extra):
         pulled = resid[p] - step * (spread[p] + extra)

time: 55.6 us -> 54.3 us (0.977)
  Pallas kernels: 55.4 us -> 54.2 us
    pallas_call x1, Pallas kernels: 54.7 us -> 53.5 us  [per_device(): pl.pallas_call(functools.partial(kernel, ny, nx), out_shape=(whole, whole...]
where the time goes in v7:
time: 54.3 us; the launch traced here: 54.2 us
  Pallas kernels  54.2 us (100%)
    pallas_call x1, Pallas kernels, per_device(): pl.pallas_call(functools.partial(kernel, ny, nx), out_shape=(whole, whole...  53.5 us

profile of v7, /device:TPU:1, one launch (start us, length us, event | category | flops | bytes accessed | tf_op | source)
XLA Modules:
  0.0 54.2 jit_solution(4541330386442392486)
XLA Ops:
  0.0 53.5 %shard_map.37 = (f32[16,32,128]{2,1,0:T(8,128)S(1)}, f32[16,32,128]{2,1,0:T(8,128)S(1)}, f32[1,128]{1,0:T(1,128)S(1)}) custom-call(f32[16,32,128]{2,1,0:T(8,128)} %obs_hbm.1, f32[9,3,64]{2,1,0:T(4,128)} %bitcast.1, s32[16,32]{1,0:T(8,128)} %tiles_hbm.1), custom_call_target="tpu_custom_call" | custom-call | tf_op jit(solution)/shard_map/pallas_call | solution.py:701
  53.5 0.7 %shard_map.38 = f32[16,32,128]{2,1,0:T(8,128)} custom-call(f32[16,32,128]{2,1,0:T(8,128)S(1)} %get-tuple-element.8.u, f32[16,32,128]{2,1,0:T(8,128)S(1)} %get-tuple-element.9.g, f32[1,128]{1,0:T(1,128)S(1)} %get-tuple-element.10.step), custom_call_target="tpu_custom_call" | custom-call | tf_op jit(solution)/shard_map/pallas_call | solution.py:711

commit v8 on v7

--- a/solution.py
+++ b/solution.py
@@ -53,7 +53,7 @@
 
     barrier = pltpu.get_barrier_semaphore()
 
-    for dy, dx in SIDES:
+    for dy, dx in SIDES[::-1]:
         pl.semaphore_signal(barrier, inc=1, device_id=at(dy, dx), device_id_type=MESH)
 
     lane = lax.broadcasted_iota(jnp.int32, (1, CX), 1)
@@ -220,6 +220,7 @@
             ext[p, pl.ds(0, 8), :] = rows[p]
             ext[p, pl.ds(8 + CY, 8), :] = rows[p]
         y_fix[...] = cross(rows, along, False, fwd)
+        packed_fix[:] = [packed_rows_fix()]
         if between is not None:
             made[2].wait_recv()
             made[3].wait_recv()
@@ -250,12 +251,15 @@
         wait_rows(made)
         rows = get_rows(recv_y.at[r, 0], recv_y.at[r, 1], first_row, last_row)
         y_fix[...] = jnp.concatenate(rows, axis=0)
+        packed_fix[:] = [packed_rows_fix()]
         wait_columns(made)
         both = sides(r, place >= 4)
         x_fix[pl.ds(0, 8), :] = both[8:16] + both[0:8]
         x_fix[pl.ds(8, 16), :] = both[16:CY]
         x_fix[pl.ds(24, 8), :] = both[CY : CY + 8] + both[CY + 8 : CY + 16]
 
+    packed_fix = []
+
     def packed_rows_fix():
         packed = jnp.zeros((8, CX), F32)
         for p in range(Z):
@@ -263,7 +267,7 @@
         return packed
 
     def fixed_columns(edge):
-        packed = packed_rows_fix()
+        packed = packed_fix[0]
         edge = edge + x_fix[...]
         top = edge[0:8] + jnp.where(low_half, packed, 0.0)
         low = edge[CY - 8 : CY] + jnp.where(low_half, 0.0, packed)

time: 54.3 us -> 54.2 us (level)
  no operation moved by 1% of the time
where the time goes in v8:
time: 54.2 us; the launch traced here: 54 us
  Pallas kernels  54 us (100%)
    pallas_call x1, Pallas kernels, per_device(): pl.pallas_call(functools.partial(kernel, ny, nx), out_shape=(whole, whole...  53.3 us

profile of v8, /device:TPU:1, one launch (start us, length us, event | category | flops | bytes accessed | tf_op | source)
XLA Modules:
  0.0 54.0 jit_solution(3262371923140360104)
XLA Ops:
  0.0 53.3 %shard_map.37 = (f32[16,32,128]{2,1,0:T(8,128)S(1)}, f32[16,32,128]{2,1,0:T(8,128)S(1)}, f32[1,128]{1,0:T(1,128)S(1)}) custom-call(f32[16,32,128]{2,1,0:T(8,128)} %obs_hbm.1, f32[9,3,64]{2,1,0:T(4,128)} %bitcast.1, s32[16,32]{1,0:T(8,128)} %tiles_hbm.1), custom_call_target="tpu_custom_call" | custom-call | tf_op jit(solution)/shard_map/pallas_call | solution.py:705
  53.3 0.7 %shard_map.38 = f32[16,32,128]{2,1,0:T(8,128)} custom-call(f32[16,32,128]{2,1,0:T(8,128)S(1)} %get-tuple-element.8.u, f32[16,32,128]{2,1,0:T(8,128)S(1)} %get-tuple-element.9.g, f32[1,128]{1,0:T(1,128)S(1)} %get-tuple-element.10.step), custom_call_target="tpu_custom_call" | custom-call | tf_op jit(solution)/shard_map/pallas_call | solution.py:715
